TPU v7x, 128 devices: a whole 4x4x4 slice. The times are simulated.
128 devices in a mesh: ctx: 32 (over z, y, core), ch: 4 (over x).
Axes of the slice: x: 4, y: 4, z: 4, core: 2. Of those that a mesh axis runs over, the one named last changes fastest.
Arguments:
- query_in: bfloat16 [5120, 8192], P('ctx', 'ch'), may hold values from -6 to 6
- key_in: bfloat16 [5120, 8192], P('ctx', 'ch'), may hold values from -6 to 6
- value_in: bfloat16 [5120, 8192], P('ctx', 'ch'), may hold values from -6 to 6
- row_place: int32 [5120], P('ctx'), may hold values from 0 to 5119, as said below
- short_weight: bfloat16 [3, 7, 8192], P(None, None, 'ch'), may hold values from -2 to 2
- long_filter: bfloat16 [128, 8192], P(None, 'ch'), may hold values from -0.5 to 0.5
- target: bfloat16 [5120, 8192], P('ctx', 'ch'), may hold values from -6 to 6
- taxon_ids: int32 [5120], P('ctx'), may hold values from 0 to 15
- taxon_weight: float32 [16], replicated, may hold values from 0.5 to 2
Outputs:
- gated_out: bfloat16 [5120, 8192], P('ctx', 'ch')
- query_grad: bfloat16 [5120, 8192], P('ctx', 'ch')
- key_grad: bfloat16 [5120, 8192], P('ctx', 'ch')
- value_grad: bfloat16 [5120, 8192], P('ctx', 'ch')
- filter_grad: float32 [128, 8192], P(None, 'ch')
- short_grad: float32 [3, 7, 8192], P(None, None, 'ch')
- taxon_loss: float32 [16], replicated
Inputs may be any that keep to these rules, and one draw needn't show every extreme that they name: row_place is a permutation of the 5120 positions. Of the 160 rows that one device of index k holds, exactly 10 have positions in the block of 160 positions of device (k + 1) mod 32, exactly 5 in the block of every other device but one, and none in the block of that one.
All inputs are finite; a program needn't handle non-finite values.
Results may differ from a plain program's by a relative error of at most 0.0052.
Values may be sent and summed in bfloat16 or wider, within the bound.
A program may use at most 320 MiB of HBM per device.

v0:
```python
import math

import jax
import jax.numpy as jnp
import numpy as np
from jax import lax
from jax.sharding import PartitionSpec as P

tile_rows = 32


def passed_along(x, axis, by):
    length = lax.axis_size(axis)
    pairs = [(i, i + by) for i in range(length) if 0 <= i + by < length]
    return lax.ppermute(x, axis, pairs)


def skew_rows(row, span_width):
    channels = row.shape[1]
    table = (np.arange(span_width)[None, :] - np.arange(tile_rows)[:, None]) % (span_width + 1)
    picked = jnp.take(row, jnp.asarray(table.reshape(-1), dtype=jnp.int32), axis=0)
    return picked.reshape(tile_rows, span_width, channels)


def forward_matrix(long_filter):
    filter_len, channels = long_filter.shape
    zero_row = jnp.zeros((1, channels), long_filter.dtype)
    tail_rows = jnp.zeros((tile_rows, channels), long_filter.dtype)
    return skew_rows(
        jnp.concatenate([zero_row, long_filter[::-1], tail_rows], axis=0), tile_rows + filter_len
    )


def backward_matrix(long_filter):
    filter_len, channels = long_filter.shape
    tail_rows = jnp.zeros((tile_rows + 1, channels), long_filter.dtype)
    return skew_rows(jnp.concatenate([long_filter, tail_rows], axis=0), tile_rows + filter_len)


def windows(padded, filter_len):
    row_total = padded.shape[0] - filter_len
    blocks = row_total // tile_rows
    pieces = [
        padded[piece_index * tile_rows : piece_index * tile_rows + row_total].reshape(
            blocks, tile_rows, padded.shape[1]
        )
        for piece_index in range(filter_len // tile_rows + 1)
    ]
    return jnp.concatenate(pieces, axis=1)


def diagonal_sums(grid_sums, filter_len):
    span_width = grid_sums.shape[1]
    channels = grid_sums.shape[2]
    flattened = grid_sums.reshape(tile_rows * span_width, channels)
    flattened = jnp.concatenate([flattened, jnp.zeros((tile_rows, channels), jnp.float32)], axis=0)
    skewed = flattened.reshape(tile_rows, span_width + 1, channels)[:, 1 : filter_len + 1]
    return jnp.sum(skewed, axis=0)[::-1]


def causal_taps(extended, weights, row_total):
    short_taps = weights.shape[0]
    summed = jnp.zeros((row_total, extended.shape[1]), jnp.float32)
    for offset in range(short_taps):
        begin_at = short_taps - 1 - offset
        summed = summed + weights[offset].astype(jnp.float32) * extended[
            begin_at : begin_at + row_total
        ].astype(jnp.float32)
    return summed


def reverse_taps(extended, weights, row_total):
    summed = jnp.zeros((row_total, extended.shape[1]), jnp.float32)
    for offset in range(weights.shape[0]):
        summed = (
            summed + weights[offset].astype(jnp.float32) * extended[offset : offset + row_total]
        )
    return summed


def tap_products(grads, extended, short_taps):
    row_total = grads.shape[0]
    rows_out = []
    for offset in range(short_taps):
        begin_at = short_taps - 1 - offset
        rows_out.append(
            jnp.sum(grads * extended[begin_at : begin_at + row_total].astype(jnp.float32), axis=0)
        )
    return jnp.stack(rows_out)


def shards(
    query_in,
    key_in,
    value_in,
    row_place,
    short_weight,
    long_filter,
    target,
    taxon_ids,
    taxon_weight,
):
    row_count, channels = query_in.shape
    peer_count = lax.axis_size("ctx")
    group_count = lax.axis_size("ch")
    filter_len = long_filter.shape[0]
    short_taps = short_weight.shape[1]
    margin = short_taps - 1
    seg_rows = row_count * peer_count
    row_ids = jnp.arange(row_count, dtype=jnp.int32)
    owner = row_place // row_count
    local_place = row_place % row_count
    owner_hot = (owner[:, None] == jnp.arange(peer_count, dtype=jnp.int32)[None, :]).astype(
        jnp.int32
    )
    owner_rank = jnp.sum(jnp.cumsum(owner_hot, axis=0) * owner_hot, axis=1) - 1
    capacity = 2 * row_count // peer_count
    slot_count = peer_count * capacity
    send_slot = owner * capacity + owner_rank
    slot_source = jnp.full((slot_count,), row_count, jnp.int32).at[send_slot].set(row_ids)
    slot_place = jnp.full((slot_count,), row_count, jnp.int32).at[send_slot].set(local_place)

    def pack_rows(rows):
        return jnp.take(rows, slot_source, axis=0, mode="fill", fill_value=0).reshape(
            peer_count, capacity, channels
        )

    got_query, got_key, got_value, got_place = (
        lax.all_to_all(pack_rows(query_in), "ctx", split_axis=0, concat_axis=0, tiled=True),
        lax.all_to_all(pack_rows(key_in), "ctx", split_axis=0, concat_axis=0, tiled=True),
        lax.all_to_all(pack_rows(value_in), "ctx", split_axis=0, concat_axis=0, tiled=True),
        lax.all_to_all(
            slot_place.reshape(peer_count, capacity), "ctx", split_axis=0, concat_axis=0, tiled=True
        ),
    )
    recv_place = got_place.reshape(slot_count)
    flat_query = got_query.reshape(slot_count, channels)
    flat_key = got_key.reshape(slot_count, channels)
    flat_value = got_value.reshape(slot_count, channels)
    place_slot = (
        jnp.zeros((row_count,), jnp.int32)
        .at[recv_place]
        .set(jnp.arange(slot_count, dtype=jnp.int32), mode="drop")
    )
    query_rows = jnp.take(flat_query, place_slot, axis=0)
    key_rows = jnp.take(flat_key, place_slot, axis=0)
    value_rows = jnp.take(flat_value, place_slot, axis=0)
    prior_query, prior_key, prior_value = passed_along(
        (
            query_rows[row_count - margin :],
            key_rows[row_count - margin :],
            value_rows[row_count - margin :],
        ),
        "ctx",
        1,
    )
    query_ext = jnp.concatenate([prior_query, query_rows], axis=0)
    key_ext = jnp.concatenate([prior_key, key_rows], axis=0)
    value_ext = jnp.concatenate([prior_value, value_rows], axis=0)
    query_conv = causal_taps(query_ext, short_weight[0], row_count)
    key_conv = causal_taps(key_ext, short_weight[1], row_count)
    value_conv = causal_taps(value_ext, short_weight[2], row_count)
    gated = (key_conv * value_conv).astype(jnp.bfloat16)
    prior_gated = passed_along(gated[row_count - filter_len + 1 :], "ctx", 1)
    gated_pad = jnp.concatenate(
        [jnp.zeros((1, channels), jnp.bfloat16), prior_gated, gated], axis=0
    )
    window_rows = windows(gated_pad, filter_len)
    mixed = jnp.einsum(
        "abc,nbc->nac", forward_matrix(long_filter), window_rows, preferred_element_type=jnp.float32
    ).reshape(row_count, channels)
    gated_out = (query_conv * mixed).astype(jnp.bfloat16)
    target_f = target.astype(jnp.float32)
    row_loss = jnp.sum(gated_out.astype(jnp.float32) * target_f, axis=1)
    taxon_count = taxon_weight.shape[0]
    taxon_hot = (taxon_ids[:, None] == jnp.arange(taxon_count, dtype=jnp.int32)[None, :]).astype(
        jnp.float32
    )
    loss_scale = 1.0 / math.sqrt(channels * group_count * seg_rows / taxon_count)
    loss_part = jnp.dot(row_loss, taxon_hot, precision=lax.Precision.HIGHEST) * loss_scale
    row_weight = jnp.dot(taxon_hot, taxon_weight, precision=lax.Precision.HIGHEST)
    grad_out = row_weight[:, None] * target_f
    grad_qconv = grad_out * mixed
    grad_mixed = (grad_out * query_conv).astype(jnp.bfloat16)
    next_mixed = passed_along(grad_mixed[: filter_len - 1], "ctx", -1)
    mixed_pad = jnp.concatenate(
        [grad_mixed, next_mixed, jnp.zeros((1, channels), jnp.bfloat16)], axis=0
    )
    grad_gated = jnp.einsum(
        "abc,nbc->nac",
        backward_matrix(long_filter),
        windows(mixed_pad, filter_len),
        preferred_element_type=jnp.float32,
    ).reshape(row_count, channels)
    grad_kconv = grad_gated * value_conv
    grad_vconv = grad_gated * key_conv
    grad_scale = 1.0 / math.sqrt(seg_rows)
    tile_grads = jnp.einsum(
        "nac,nbc->abc",
        grad_mixed.reshape(-1, tile_rows, channels),
        window_rows,
        preferred_element_type=jnp.float32,
    )
    filter_part = diagonal_sums(tile_grads, filter_len) * grad_scale
    short_part = (
        jnp.stack(
            [
                tap_products(grad_qconv, query_ext, short_taps),
                tap_products(grad_kconv, key_ext, short_taps),
                tap_products(grad_vconv, value_ext, short_taps),
            ]
        )
        * grad_scale
    )
    next_query, next_key, next_value = passed_along(
        (grad_qconv[:margin], grad_kconv[:margin], grad_vconv[:margin]), "ctx", -1
    )
    grad_query = reverse_taps(
        jnp.concatenate([grad_qconv, next_query], axis=0), short_weight[0], row_count
    ).astype(jnp.bfloat16)
    grad_key = reverse_taps(
        jnp.concatenate([grad_kconv, next_key], axis=0), short_weight[1], row_count
    ).astype(jnp.bfloat16)
    grad_value = reverse_taps(
        jnp.concatenate([grad_vconv, next_value], axis=0), short_weight[2], row_count
    ).astype(jnp.bfloat16)
    filter_grad, short_grad = lax.psum((filter_part, short_part), "ctx")
    taxon_loss = lax.psum(loss_part, ("ctx", "ch"))

    def return_rows(rows):
        return jnp.take(rows, recv_place, axis=0, mode="fill", fill_value=0)

    back_query, back_key, back_value = (
        lax.all_to_all(
            return_rows(grad_query).reshape(peer_count, capacity, channels),
            "ctx",
            split_axis=0,
            concat_axis=0,
            tiled=True,
        ),
        lax.all_to_all(
            return_rows(grad_key).reshape(peer_count, capacity, channels),
            "ctx",
            split_axis=0,
            concat_axis=0,
            tiled=True,
        ),
        lax.all_to_all(
            return_rows(grad_value).reshape(peer_count, capacity, channels),
            "ctx",
            split_axis=0,
            concat_axis=0,
            tiled=True,
        ),
    )
    flat_back_query = back_query.reshape(slot_count, channels)
    flat_back_key = back_key.reshape(slot_count, channels)
    flat_back_value = back_value.reshape(slot_count, channels)
    return (
        gated_out,
        jnp.take(flat_back_query, send_slot, axis=0),
        jnp.take(flat_back_key, send_slot, axis=0),
        jnp.take(flat_back_value, send_slot, axis=0),
        filter_grad,
        short_grad,
        taxon_loss,
    )


def solution(mesh):
    placed = (
        P("ctx", "ch"),
        P("ctx", "ch"),
        P("ctx", "ch"),
        P("ctx"),
        P(None, None, "ch"),
        P(None, "ch"),
        P("ctx", "ch"),
        P("ctx"),
        P(),
    )
    return jax.shard_map(
        shards,
        mesh=mesh,
        in_specs=placed,
        out_specs=(
            P("ctx", "ch"),
            P("ctx", "ch"),
            P("ctx", "ch"),
            P("ctx", "ch"),
            P(None, "ch"),
            P(None, None, "ch"),
            P(),
        ),
        check_vma=False,
    )
```

profile of v0, /device:TPU:1, one launch (start us, length us, event | category | flops | bytes accessed | tf_op | source)
XLA Modules:
  0.0 787.2 jit_solution(2346542402354719930)
XLA Ops:
  11.3 9.6 %all-to-all-start.1 = ((s32[32,1,10]{2,1,0:T(1,128)}), s32[32,1,10]{2,1,0:T(1,128)S(1)}, u32[]{:S(2)}, u32[]{:S(2)}) async-start(s32[32,1,10]{2,1,0:T(1,128)} %bitcast.2), calls=%async_computation.1 | async-start | bytes 32768 | tf_op jit(solution)/shard_map/all_to_all | solution.py:132
  22.1 2.4 gather_fusion.2
  24.6 3.0 gather_fusion.4
  27.6 3.0 gather_fusion
  30.6 3.8 broadcast_select_fusion.4
  34.5 3.3 reshape.361
  37.8 7.4 all-to-all-start.2
  45.2 3.3 reshape.363
  48.5 25.3 %all-to-all-done.2 = bf16[32,10,2048]{2,1,0:T(8,128)(2,1)S(1)} async-done(((bf16[32,10,2048]{2,1,0:T(8,128)(2,1)}), bf16[32,10,2048]{2,1,0:T(8,128)(2,1)S(1)}, u32[]{:S(2)}, u32[]{:S(2)}) %all-to-all-start.2) | async-done | bytes 1310752 | tf_op jit(solution)/shard_map/all_to_all | solution.py:130
  75.1 6.1 all-to-all-start.3
  81.2 3.4 reshape.358
  86.7 22.8 %all-to-all-done.3 = bf16[32,10,2048]{2,1,0:T(8,128)(2,1)} async-done(((bf16[32,10,2048]{2,1,0:T(8,128)(2,1)}), bf16[32,10,2048]{2,1,0:T(8,128)(2,1)}, u32[]{:S(2)}, u32[]{:S(2)}) %all-to-all-start.3) | async-done | bytes 1310752 | tf_op jit(solution)/shard_map/all_to_all | solution.py:131
  109.5 6.5 all-to-all-start
  117.7 3.1 scatter_custom_fusion.2
  120.8 2.5 reshape.362
  125.2 2.5 reshape.364
  129.6 14.8 %all-to-all-done = bf16[32,10,2048]{2,1,0:T(8,128)(2,1)} async-done(((bf16[32,10,2048]{2,1,0:T(8,128)(2,1)}), bf16[32,10,2048]{2,1,0:T(8,128)(2,1)}, u32[]{:S(2)}, u32[]{:S(2)}) %all-to-all-start) | async-done | bytes 1310752 | tf_op jit(solution)/shard_map/all_to_all | solution.py:129
  144.3 2.5 reshape.359
  150.6 3.3 collective-permute-start
  154.2 25.8 %gather_fusion.9 = bf16[5120,2048]{1,0:T(8,128)(2,1)} fusion(bf16[161,2048]{1,0:T(8,128)(2,1)S(1)} %concatenate.60, s32[5120]{0:T(1024)S(1)} %broadcast_clamp_fusion), kind=kCustom, calls=%fused_computation.13.clone | custom fusion | bytes 41963520 | tf_op jit(solution)/shard_map/jit(_take)/gather | solution.py:21
  180.0 47.8 %copy.59 = bf16[32,160,2048]{1,0,2:T(8,128)(2,1)} copy(bf16[32,160,2048]{2,1,0:T(8,128)(2,1)} %bitcast.107) | data formatting | bytes 41943040 | tf_op jit(solution)/shard_map/reshape | solution.py:22
  227.8 25.8 %gather_fusion.6 = bf16[5120,2048]{1,0:T(8,128)(2,1)} fusion(bf16[161,2048]{1,0:T(8,128)(2,1)S(1)} %maximum_maximum_fusion, s32[5120]{0:T(1024)S(1)} %broadcast_clamp_fusion), kind=kCustom, calls=%fused_computation.2.clone | custom fusion | bytes 41963520 | tf_op jit(solution)/shard_map/jit(_take)/gather | solution.py:21
  253.6 47.8 %copy.56 = bf16[32,160,2048]{1,0,2:T(8,128)(2,1)} copy(bf16[32,160,2048]{2,1,0:T(8,128)(2,1)} %bitcast.106) | data formatting | bytes 41943040 | tf_op jit(solution)/shard_map/reshape | solution.py:22
  301.6 2.2 fusion.2
  303.8 2.1 collective-permute-start.5
  306.5 3.5 collective-permute-start.2
  318.3 10.3 %copy.58 = bf16[5,160,2048]{1,0,2:T(8,128)(2,1)} copy(bf16[5,160,2048]{2,1,0:T(8,128)(2,1)} %constant_dynamic-update-slice_fusion.5) | data formatting | bytes 6553600 | tf_op jit(solution)/shard_map/concatenate | solution.py:49
  328.7 19.8 %convolution_bitcast_fusion.1 = f32[5,32,2048]{1,0,2:T(8,128)} fusion(bf16[5,160,2048]{1,0,2:T(8,128)(2,1)} %copy.58, bf16[32,160,2048]{1,0,2:T(8,128)(2,1)} %copy.59), kind=kOutput, calls=%fused_computation.34 | convolution fusion | flops 104857600 | bytes 25559040 | tf_op jit(solution)/shard_map/abc,nbc->nac/dot_general | solution.py:189
  348.5 4.8 copy.60
  353.5 3.4 fusion.41
  357.0 3.4 fusion.28
  360.7 1.9 collective-permute-start.3
  362.7 2.6 collective-permute-start.7
  365.4 1.9 collective-permute-start.6
  374.5 10.3 %copy.55 = bf16[5,160,2048]{1,0,2:T(8,128)(2,1)} copy(bf16[5,160,2048]{2,1,0:T(8,128)(2,1)} %constant_dynamic-update-slice_fusion) | data formatting | bytes 6553600 | tf_op jit(solution)/shard_map/concatenate | solution.py:49
  384.9 19.8 %convolution_bitcast_fusion.2 = f32[5,32,2048]{1,0,2:T(8,128)} fusion(bf16[5,160,2048]{1,0,2:T(8,128)(2,1)} %copy.55, bf16[32,160,2048]{1,0,2:T(8,128)(2,1)} %copy.56), kind=kOutput, calls=%fused_computation.35 | convolution fusion | flops 104857600 | bytes 25559040 | tf_op jit(solution)/shard_map/abc,nbc->nac/dot_general | solution.py:169
  404.7 5.8 copy.57
  410.5 4.4 fusion.15
  414.9 1.9 collective-permute-start.4
  418.3 3.0 gather_fusion.12
  421.3 3.0 gather_fusion.10
  424.3 5.4 fusion.81
  429.7 3.0 gather_fusion.7
  432.8 4.2 broadcast_select_fusion
  437.0 3.3 reshape.384
  440.3 11.8 %all-to-all-start.6 = ((bf16[32,10,2048]{2,1,0:T(8,128)(2,1)}), bf16[32,10,2048]{2,1,0:T(8,128)(2,1)}, u32[]{:S(2)}, u32[]{:S(2)}) async-start(bf16[32,10,2048]{2,1,0:T(8,128)(2,1)} %reshape.384), calls=%async_computation.6 | async-start | bytes 4194304 | tf_op jit(solution)/shard_map/all_to_all | solution.py:248
  452.2 4.3 copy.62
  456.8 3.3 reshape.382
  460.2 20.4 %all-to-all-done.6 = bf16[32,10,2048]{2,1,0:T(8,128)(2,1)} async-done(((bf16[32,10,2048]{2,1,0:T(8,128)(2,1)}), bf16[32,10,2048]{2,1,0:T(8,128)(2,1)}, u32[]{:S(2)}, u32[]{:S(2)}) %all-to-all-start.6) | async-done | bytes 1310752 | tf_op jit(solution)/shard_map/all_to_all | solution.py:248
  480.6 5.3 all-to-all-start.5
  485.9 27.7 %convolution_bitcast_fusion = f32[32,160,2048]{1,0,2:T(8,128)} fusion(bf16[5,160,2048]{1,0,2:T(8,128)(2,1)} %copy.55, bf16[5,32,2048]{1,0,2:T(8,128)(2,1)} %copy.62), kind=kOutput, calls=%fused_computation.18 | convolution fusion | flops 104857600 | bytes 45875200 | tf_op jit(solution)/shard_map/nac,nbc->abc/dot_general | solution.py:198
  513.6 61.3 %copy.63 = f32[32,160,2048]{2,1,0:T(8,128)} copy(f32[32,160,2048]{1,0,2:T(8,128)} %convolution_bitcast_fusion) | data formatting | bytes 83886080 | tf_op jit(solution)/shard_map/nac,nbc->abc/transpose | solution.py:198
  575.0 29.6 %concatenate.63 = f32[5152,2048]{1,0:T(8,128)} pad(f32[5120,2048]{1,0:T(8,128)} %bitcast.105, f32[]{:T(128)} %constant.54.clone.1), padding=0_32x0_0 | pad | bytes 84148224 | tf_op jit(solution)/shard_map/concatenate | solution.py:56
  604.5 37.5 %reshape.387 = f32[32,161,2048]{2,1,0:T(8,128)} reshape(f32[5152,2048]{1,0:T(8,128)} %concatenate.63) | data formatting | bytes 84410368 | tf_op jit(solution)/shard_map/reshape | solution.py:57
  642.0 3.3 reshape.373
  646.6 7.5 all-to-all-start.4
  654.2 13.1 %slice_reduce_fusion = f32[128,2048]{1,0:T(8,128)S(1)} fusion(f32[32,161,2048]{2,1,0:T(8,128)} %reshape.387), kind=kLoop, calls=%fused_computation.17 | loop fusion | flops 8126464 | bytes 34603008 | tf_op jit(solution)/shard_map/reduce_sum | solution.py:58
  671.0 67.3 %psum.23 = f32[16]{0:T(128)} all-reduce(f32[16]{0:T(128)S(1)} %fusion.98), channel_id=1, replica_groups=mesh['ctx'=32,'ch'=4] {'ctx','ch'}, use_global_device_ids=true, to_apply=%region_31.35 | all-reduce | flops 16 | bytes 128 | tf_op jit(solution)/shard_map/psum | solution.py:228
  738.3 2.5 reshape.385
  741.9 2.5 reshape.383
  745.5 2.5 reshape.374
  749.9 2.5 broadcast_select_fusion.6
  752.4 24.7 %all-reduce.6.cloned.1.call-done = (f32[128,2048]{1,0:T(8,128)}, f32[3,7,2048]{2,1,0:T(8,128)}) async-done(((f32[128,2048]{1,0:T(8,128)}, f32[3,7,2048]{2,1,0:T(8,128)}), (f32[128,2048]{1,0:T(8,128)}, f32[3,7,2048]{2,1,0:T(8,128)})) %all-reduce.6.cloned.1.call-update) | async-done | bytes 1220624 | tf_op jit(solution)/shard_map/psum | solution.py:227
  777.1 2.3 copy.78
  (227 shorter events, 45.9 us)
Async XLA Ops:
  7.2 14.9 %copy-start = (bf16[160,2048]{1,0:T(8,128)(2,1)S(1)}, bf16[160,2048]{1,0:T(8,128)(2,1)}, u32[]{:S(2)}) copy-start(bf16[160,2048]{1,0:T(8,128)(2,1)} %param.18) | copy-start | bytes 1966084
  9.5 12.5 %copy-start.60 = (s32[160]{0:T(256)}, s32[160]{0:T(256)S(1)}, u32[]{:S(2)}) copy-start(s32[160]{0:T(256)S(1)} %get-tuple-element.41) | copy-start | bytes 1924
  11.3 26.4 %all-to-all-start.1 = ((s32[32,1,10]{2,1,0:T(1,128)}), s32[32,1,10]{2,1,0:T(1,128)S(1)}, u32[]{:S(2)}, u32[]{:S(2)}) async-start(s32[32,1,10]{2,1,0:T(1,128)} %bitcast.2), calls=%async_computation.1 | async-start | bytes 32768 | tf_op jit(solution)/shard_map/all_to_all | solution.py:132
  37.8 36.0 %all-to-all-start.2 = ((bf16[32,10,2048]{2,1,0:T(8,128)(2,1)}), bf16[32,10,2048]{2,1,0:T(8,128)(2,1)S(1)}, u32[]{:S(2)}, u32[]{:S(2)}) async-start(bf16[32,10,2048]{2,1,0:T(8,128)(2,1)} %reshape.361), calls=%async_computation.2 | async-start | bytes 4194304 | tf_op jit(solution)/shard_map/all_to_all | solution.py:130
  75.1 34.4 %all-to-all-start.3 = ((bf16[32,10,2048]{2,1,0:T(8,128)(2,1)}), bf16[32,10,2048]{2,1,0:T(8,128)(2,1)}, u32[]{:S(2)}, u32[]{:S(2)}) async-start(bf16[32,10,2048]{2,1,0:T(8,128)(2,1)} %reshape.363), calls=%async_computation.3 | async-start | bytes 4194304 | tf_op jit(solution)/shard_map/all_to_all | solution.py:131
  81.2 4.2 copy-start.20
  86.7 29.3 %copy-start.57 = (s32[5120]{0:T(1024)S(1)}, s32[5120]{0:T(1024)}, u32[]{:S(2)}) copy-start(s32[5120]{0:T(1024)} %constant.105) | copy-start | bytes 61444
  109.5 34.8 %all-to-all-start = ((bf16[32,10,2048]{2,1,0:T(8,128)(2,1)}), bf16[32,10,2048]{2,1,0:T(8,128)(2,1)}, u32[]{:S(2)}, u32[]{:S(2)}) async-start(bf16[32,10,2048]{2,1,0:T(8,128)(2,1)} %reshape.358), calls=%async_computation | async-start | bytes 4194304 | tf_op jit(solution)/shard_map/all_to_all | solution.py:129
  148.7 5.1 copy-start.64
  148.7 5.1 copy-start.66
  148.7 5.3 copy-start.19
  150.5 151.0 %copy-start.6 = (bf16[160,2048]{1,0:T(8,128)(2,1)}, bf16[160,2048]{1,0:T(8,128)(2,1)S(1)}, u32[]{:S(2)}) copy-start(bf16[160,2048]{1,0:T(8,128)(2,1)S(1)} %get-tuple-element.82) | copy-start | bytes 1966084
  150.5 155.9 %copy-start.10 = (bf16[160,2048]{1,0:T(8,128)(2,1)}, bf16[160,2048]{1,0:T(8,128)(2,1)S(1)}, u32[]{:S(2)}) copy-start(bf16[160,2048]{1,0:T(8,128)(2,1)S(1)} %get-tuple-element.81) | copy-start | bytes 1966084
  150.5 159.4 %copy-start.8 = (bf16[160,2048]{1,0:T(8,128)(2,1)}, bf16[160,2048]{1,0:T(8,128)(2,1)S(1)}, u32[]{:S(2)}) copy-start(bf16[160,2048]{1,0:T(8,128)(2,1)S(1)} %get-tuple-element.80) | copy-start | bytes 1966084
  150.6 151.0 %collective-permute-start = (bf16[6,2048]{1,0:T(8,128)(2,1)S(1)}, bf16[6,2048]{1,0:T(8,128)(2,1)S(1)}, u32[]{:S(2)}, u32[]{:S(2)}) collective-permute-start(bf16[6,2048]{1,0:T(8,128)(2,1)S(1)} %slice.431), channel_id=1, source_target_pairs={{0,4},{4,8},{8,12},{12,16},{16,20},{20,24},{24,28},{28,32},{32,36}... | collective-permute-start | bytes 73736 | tf_op jit(solution)/shard_map/ppermute | solution.py:15
  154.1 147.5 %copy-start.58 = (f32[1,160]{1,0:T(1,128)}, f32[1,160]{1,0:T(1,128)S(1)}, u32[]{:S(2)}) copy-start(f32[1,160]{1,0:T(1,128)S(1)} %fusion.118) | copy-start | bytes 1924
  253.6 47.9 %copy-start.12 = (bf16[160,2048]{1,0:T(8,128)(2,1)S(1)}, bf16[160,2048]{1,0:T(8,128)(2,1)}, u32[]{:S(2)}) copy-start(bf16[160,2048]{1,0:T(8,128)(2,1)} %param.23) | copy-start | bytes 1966084
  303.8 10.5 %collective-permute-start.5 = (bf16[127,2048]{1,0:T(8,128)(2,1)S(1)}, bf16[127,2048]{1,0:T(8,128)(2,1)S(1)}, u32[]{:S(2)}, u32[]{:S(2)}) collective-permute-start(bf16[127,2048]{1,0:T(8,128)(2,1)S(1)} %slice.480), channel_id=1, source_target_pairs={{4,0},{8,4},{12,8},{16,12},{20,16},{24,20},{28,24},{32,28},{36,32}... | collective-permute-start | bytes 1560584 | tf_op jit(solution)/shard_map/ppermute | solution.py:15
  306.5 46.9 %collective-permute-start.2 = (bf16[6,2048]{1,0:T(8,128)(2,1)S(1)}, bf16[6,2048]{1,0:T(8,128)(2,1)S(1)}, u32[]{:S(2)}, u32[]{:S(2)}) collective-permute-start(bf16[6,2048]{1,0:T(8,128)(2,1)S(1)} %slice.453), channel_id=1, source_target_pairs={{0,4},{4,8},{8,12},{12,16},{16,20},{20,24},{24,28},{28,32},{32,36}... | collective-permute-start | bytes 73736 | tf_op jit(solution)/shard_map/ppermute | solution.py:15
  310.6 42.8 %collective-permute-start.1 = (bf16[6,2048]{1,0:T(8,128)(2,1)}, bf16[6,2048]{1,0:T(8,128)(2,1)S(1)}, u32[]{:S(2)}, u32[]{:S(2)}) collective-permute-start(bf16[6,2048]{1,0:T(8,128)(2,1)} %slice.442), channel_id=1, source_target_pairs={{0,4},{4,8},{8,12},{12,16},{16,20},{20,24},{24,28},{28,32},{32,36}... | collective-permute-start | bytes 73736 | tf_op jit(solution)/shard_map/ppermute | solution.py:15
  348.5 4.9 copy-start.9
  348.5 4.9 copy-start.11
  348.5 4.9 copy-start.22
  348.5 4.9 copy-start.23
  348.5 4.9 copy-start.24
  348.5 4.9 copy-start.25
  348.5 4.9 copy-start.26
  348.5 4.9 copy-start.27
  348.5 4.9 copy-start.28
  353.5 3.5 copy-start.29
  353.5 3.5 copy-start.30
  353.5 3.5 copy-start.31
  353.5 3.5 copy-start.32
  353.5 3.5 copy-start.33
  353.5 3.5 copy-start.34
  353.5 3.5 copy-start.35
  360.5 4.9 copy-start.14
  360.7 8.9 %collective-permute-start.3 = (bf16[127,2048]{1,0:T(8,128)(2,1)S(1)}, bf16[127,2048]{1,0:T(8,128)(2,1)S(1)}, u32[]{:S(2)}, u32[]{:S(2)}) collective-permute-start(bf16[127,2048]{1,0:T(8,128)(2,1)S(1)} %slice.464), channel_id=1, source_target_pairs={{0,4},{4,8},{8,12},{12,16},{16,20},{20,24},{24,28},{28,32},{32,36}... | collective-permute-start | bytes 1560584 | tf_op jit(solution)/shard_map/ppermute | solution.py:15
  362.7 5.6 collective-permute-start.7
  365.4 51.4 %collective-permute-start.6 = (f32[6,2048]{1,0:T(8,128)S(1)}, f32[6,2048]{1,0:T(8,128)S(1)}, u32[]{:S(2)}, u32[]{:S(2)}) collective-permute-start(f32[6,2048]{1,0:T(8,128)S(1)} %slice.485), channel_id=1, source_target_pairs={{4,0},{8,4},{12,8},{16,12},{20,16},{24,20},{28,24},{32,28},{36,32}... | collective-permute-start | bytes 147464 | tf_op jit(solution)/shard_map/ppermute | solution.py:15
  404.7 5.8 copy-start.7
  404.7 5.8 copy-start.13
  404.7 5.8 copy-start.59
  410.5 6.3 copy-start.15
  414.9 9.4 %collective-permute-start.4 = (f32[6,2048]{1,0:T(8,128)S(1)}, f32[6,2048]{1,0:T(8,128)S(1)}, u32[]{:S(2)}, u32[]{:S(2)}) collective-permute-start(f32[6,2048]{1,0:T(8,128)S(1)} %slice.469), channel_id=1, source_target_pairs={{4,0},{8,4},{12,8},{16,12},{20,16},{24,20},{28,24},{32,28},{36,32}... | collective-permute-start | bytes 147464 | tf_op jit(solution)/shard_map/ppermute | solution.py:15
  440.3 40.3 %all-to-all-start.6 = ((bf16[32,10,2048]{2,1,0:T(8,128)(2,1)}), bf16[32,10,2048]{2,1,0:T(8,128)(2,1)}, u32[]{:S(2)}, u32[]{:S(2)}) async-start(bf16[32,10,2048]{2,1,0:T(8,128)(2,1)} %reshape.384), calls=%async_computation.6 | async-start | bytes 4194304 | tf_op jit(solution)/shard_map/all_to_all | solution.py:248
  452.1 4.4 copy-start.36
  452.1 4.4 copy-start.37
  452.1 4.4 copy-start.38
  452.1 4.4 copy-start.39
  452.1 4.4 copy-start.40
  452.2 4.4 copy-start.41
  452.2 4.4 copy-start.42
  452.2 4.5 copy-start.43
  452.2 4.5 copy-start.44
  452.2 4.5 copy-start.45
  452.2 4.5 copy-start.46
  452.2 4.5 copy-start.47
  452.2 4.5 copy-start.48
  452.2 4.5 copy-start.49
  480.6 164.8 %all-to-all-start.5 = ((bf16[32,10,2048]{2,1,0:T(8,128)(2,1)}), bf16[32,10,2048]{2,1,0:T(8,128)(2,1)S(1)}, u32[]{:S(2)}, u32[]{:S(2)}) async-start(bf16[32,10,2048]{2,1,0:T(8,128)(2,1)} %reshape.382), calls=%async_computation.5 | async-start | bytes 4194304 | tf_op jit(solution)/shard_map/all_to_all | solution.py:241
  646.6 98.8 %all-to-all-start.4 = ((bf16[32,10,2048]{2,1,0:T(8,128)(2,1)}), bf16[32,10,2048]{2,1,0:T(8,128)(2,1)}, u32[]{:S(2)}, u32[]{:S(2)}) async-start(bf16[32,10,2048]{2,1,0:T(8,128)(2,1)} %reshape.373), calls=%async_computation.4 | async-start | bytes 4194304 | tf_op jit(solution)/shard_map/all_to_all | solution.py:234
  654.2 123.0 %all-reduce.6.cloned.1.call-start = ((), (), s32[]{:S(2)}) async-start(), calls=%async_computation.7 | async-start | bytes 2490368 | tf_op jit(solution)/shard_map/psum | solution.py:227
  749.9 30.3 %copy-start.1 = (bf16[160,2048]{1,0:T(8,128)(2,1)S(1)}, bf16[160,2048]{1,0:T(8,128)(2,1)}, u32[]{:S(2)}) copy-start(bf16[160,2048]{1,0:T(8,128)(2,1)} %param.18) | copy-start | bytes 1966084
  (19 other events, 28.7 us)
Sparse Core Ops, SparseCore 0:
  670.2 106.9 all-reduce.5
where the time goes:
time: 800 us; the launch traced here: 787 us
  local copies, waits for them, and re-layouts  398 us (50%)
  waiting for transfers between devices  110 us (14%)
  starting transfers between devices  73.4 us (9%)
  matrix products  67.7 us (8%)
  blocking collectives  67.3 us (8%)
  other arithmetic  55 us (7%)
  between operations  15.5 us (2%)
    reshape x2, local copies, waits for them, and re-layouts, skew_rows(): return picked.reshape(tile_rows, span_width, channels)  95.6 us
    psum x1, blocking collectives, shards(): taxon_loss = lax.psum(loss_part, ('ctx', 'ch'))  67.3 us
    transpose x1, local copies, waits for them, and re-layouts, shards(): jnp.einsum('nac,nbc->abc', grad_mixed.reshape(-1, tile_rows, channels), w...  61.3 us
    gather x2, local copies, waits for them, and re-layouts, skew_rows(): jnp.take(row, jnp.asarray(table.reshape(-1), dtype=jnp.int32), axis=0)  51.7 us
    reshape x1, local copies, waits for them, and re-layouts, diagonal_sums(): flattened.reshape(tile_rows, span_width + 1, channels)[:, 1:filter_len + 1]  37.5 us
    concatenate x1, local copies, waits for them, and re-layouts, diagonal_sums(): jnp.concatenate([flattened, jnp.zeros((tile_rows, channels), jnp.float32)...  29.6 us
    dot_general x1, matrix products, shards(): jnp.einsum('nac,nbc->abc', grad_mixed.reshape(-1, tile_rows, channels), w...  27.7 us
    all_to_all x1, waiting for transfers between devices, shards(): lax.all_to_all(pack_rows(key_in), 'ctx', split_axis=0, concat_axis=0, til...  25.3 us
  transfers between devices with their start and end apart: 16, of which 7 were waited for; matrix products, arithmetic and copies ran while one was open for 61% of the time, Pallas kernels for 0%

commit v1 on v0

v1 whole, which is shorter than its diff:
```python
import math

import jax
import jax.numpy as jnp
import numpy as np
from jax import lax
from jax.experimental import pallas as pl
from jax.experimental.pallas import tpu as pltpu
from jax.sharding import PartitionSpec as P

MESH = pl.DeviceIdType.MESH
F32 = jnp.float32
BF16 = jnp.bfloat16
unit = 5
block_rows = 16
lanes = 128
edge = 16
chunks = 4
stream_step = 1024.0


def split_constant(array):
    high = array.astype(np.float32).astype(jnp.bfloat16)
    low = (array - high.astype(np.float64)).astype(np.float32).astype(jnp.bfloat16)
    return high, low


def dft_tables(rows, taps):
    half = rows
    size = 2 * rows
    span = taps + rows + edge
    theta = np.pi * (2 * np.arange(half) + 1) / size

    def ahead(index):
        angle = theta[:, None] * index[None, :]
        return np.concatenate([np.cos(angle), -np.sin(angle)], axis=0)

    def back(index):
        angle = theta[None, :] * index[:, None]
        return np.concatenate([np.cos(angle), -np.sin(angle)], axis=1) * (2.0 / size)

    tables = {
        "ahead": ahead(np.arange(span)),
        "own": ahead(np.arange(rows)),
        "later": ahead(np.arange(rows, rows + taps + edge)),
        "taps": ahead(np.arange(taps)),
        "mixed": back(np.arange(rows + edge) + taps),
        "gated": back(np.arange(rows + edge)),
        "filter": back(taps - np.arange(taps)),
    }
    return tables


table_names = ("ahead", "own", "later", "taps", "mixed", "gated", "filter")


def payload_rows(taps, short_taps):
    return -(-(taps + 3 * short_taps) // 32) * 32


def iota(shape, axis):
    return lax.broadcasted_iota(jnp.int32, shape, axis)


def slot_facts(index):
    block = lax.shift_right_logical(index, 4)
    row = jnp.bitwise_and(index, block_rows - 1)
    stream = jnp.where(row >= unit, 1, 0) + jnp.where(row >= 2 * unit, 1, 0)
    rank = row - unit * stream
    valid = row < 3 * unit
    return block, stream, rank, valid


def whole_kernel(
    peers,
    groups,
    q_ref,
    k_ref,
    v_ref,
    place_ref,
    place3_ref,
    short_ref,
    filter_ref,
    target_ref,
    taxon_ref,
    weight_ref,
    ahead_hi,
    ahead_lo,
    own_hi,
    own_lo,
    later_hi,
    later_lo,
    taps_hi,
    taps_lo,
    mixed_hi,
    mixed_lo,
    gated_hi,
    gated_lo,
    filter_hi,
    filter_lo,
    out_ref,
    qg_ref,
    kg_ref,
    vg_ref,
    fg_ref,
    sg_ref,
    loss_ref,
    pack_m,
    unpack_m,
    place_m,
    return_m,
    send_b,
    recv_b,
    meta_s,
    meta_r,
    bsend_b,
    brecv_b,
    rows_b,
    prev_s,
    prev_r,
    next_s,
    next_r,
    tnext_s,
    tnext_r,
    wnext_s,
    wnext_r,
    qc_b,
    kc_b,
    vc_b,
    go_b,
    gext_b,
    gm_b,
    spec_b,
    short_b,
    gbuf,
    gr_b,
    lacc,
    par_b,
    rs_s,
    rs_r,
    ag_s,
    ag_r,
    lch_s,
    lch_r,
    lct_s,
    lct_r,
    sem_as,
    sem_ar,
    sem_bs,
    sem_br,
    sem_ps,
    sem_pr,
    sem_ns,
    sem_nr,
    sem_gs,
    sem_gr,
    sem_ms,
    sem_mr,
    sem_x,
):
    rows, channels = q_ref.shape
    taps = filter_ref.shape[0]
    short_taps = short_ref.shape[1]
    width = channels // chunks
    col_tiles = channels // lanes
    tiles = width // lanes
    pairs = tiles // 2
    blocks = peers + 1
    slots = blocks * block_rows
    ext = rows + edge
    payload = payload_rows(taps, short_taps)
    half_rows = payload // 2
    me = lax.axis_index("ctx")
    ch = lax.axis_index("ch")
    right = lax.rem(me + 1, peers)
    left = lax.rem(me + peers - 1, peers)
    grad_scale = 1.0 / math.sqrt(rows * peers)
    loss_scale = 1.0 / math.sqrt(channels * groups * rows * peers / weight_ref.shape[1])

    barrier = pltpu.get_barrier_semaphore()

    def greet(step, carry):
        pl.semaphore_signal(
            barrier, inc=1, device_id=(lax.rem(me + step, peers), ch), device_id_type=MESH
        )
        return carry

    lax.fori_loop(1, peers, greet, 0)
    for step in range(1, groups):
        pl.semaphore_signal(
            barrier, inc=1, device_id=(me, lax.rem(ch + step, groups)), device_id_type=MESH
        )

    def push(src, dst, send_sem, recv_sem, ctx_to, ch_to):
        return pltpu.make_async_remote_copy(
            src_ref=src,
            dst_ref=dst,
            send_sem=send_sem,
            recv_sem=recv_sem,
            device_id=(ctx_to, ch_to),
            device_id_type=MESH,
        )

    def drain(ref, sem):
        pltpu.make_async_copy(ref, ref, sem).wait()

    def column(row_vector, count):
        eye = iota((count, count), 0) == iota((count, count), 1)
        return jnp.sum(jnp.where(eye, row_vector, 0.0), axis=1, keepdims=True)

    place_row = place_ref[...].astype(F32)
    place3_row = place3_ref[...].astype(F32)
    owner_row = jnp.floor((place_row + 0.5) * (1.0 / rows))
    owner3_row = jnp.floor((place3_row + 0.5) * (1.0 / rows))
    owner_col = column(owner_row, rows)
    place_col = column(place_row, rows)
    local_col = place_col - owner_col * rows

    def slot_key(owner, rank):
        return jnp.where(
            rank < unit - 0.5, owner * unit + rank, float(peers * unit) + rank - unit
        )

    order3 = iota((rows, 3 * rows), 1)
    stream3 = jnp.where(order3 >= rows, 1, 0) + jnp.where(order3 >= 2 * rows, 1, 0)
    before3 = iota((rows, 3 * rows), 0) < order3 - rows * stream3
    rank3_row = jnp.sum(
        jnp.where(jnp.logical_and(owner_col == owner3_row, before3), 1.0, 0.0),
        axis=0,
        keepdims=True,
    )
    key3_row = slot_key(owner3_row, rank3_row)
    before = iota((rows, rows), 1) < iota((rows, rows), 0)
    rank_col = jnp.sum(
        jnp.where(jnp.logical_and(owner_col == owner_row, before), 1.0, 0.0),
        axis=1,
        keepdims=True,
    )
    key_col = slot_key(owner_col, rank_col)

    lane3 = iota((1, 3 * rows), 1)
    lane_stream = jnp.where(lane3 >= rows, 1, 0) + jnp.where(lane3 >= 2 * rows, 1, 0)
    lane_local = lane3 - rows * lane_stream

    def static_key(shape, axis):
        block, stream, rank, valid = slot_facts(iota(shape, axis))
        key = jnp.where(valid, stream * 1024 + block * unit + rank, -1)
        return key.astype(F32), jnp.where(valid, stream * 1024, -4096).astype(F32)

    slot_key_col, slot_stream_col = static_key((slots, 1), 0)
    slot_key_row, slot_stream_row = static_key((1, slots), 1)
    full3_row = key3_row + lane_stream.astype(F32) * stream_step
    pack_m[...] = jnp.where(slot_key_col == full3_row, 1.0, 0.0).astype(BF16)
    for s in range(3):
        return_m[s * rows : (s + 1) * rows, :] = jnp.where(
            key_col + s * stream_step == slot_key_row, 1.0, 0.0
        ).astype(BF16)

    meta_col = jnp.broadcast_to(local_col + 1.0, (rows, lanes)).astype(BF16)
    meta3 = jnp.concatenate([meta_col] * 3, axis=0)
    meta_s[...] = (
        jnp.dot(pack_m[...], meta3, preferred_element_type=F32)
        .astype(BF16)
        .reshape(blocks, block_rows, lanes)
    )

    pair_lanes = 2 * lanes

    def pack(c, carry):
        def body(u, inner):
            base = pl.multiple_of(c * width + u * pair_lanes, pair_lanes)
            cols = pl.ds(base, pair_lanes)
            stacked = jnp.concatenate([q_ref[:, cols], k_ref[:, cols], v_ref[:, cols]], axis=0)
            packed = jnp.dot(pack_m[...], stacked, preferred_element_type=F32).astype(BF16)
            local = pl.ds(pl.multiple_of(u * pair_lanes, pair_lanes), pair_lanes)
            send_b[c, :, :, local] = packed.reshape(blocks, block_rows, pair_lanes)
            return inner

        lax.fori_loop(0, pairs, body, 0)
        return carry

    ids_row = taxon_ref[...].astype(F32)
    ids_col = column(ids_row, rows)
    count = weight_ref.shape[1]
    taxon_hot = iota((rows, lanes), 1).astype(F32) == ids_col
    weights = jnp.concatenate([weight_ref[...], jnp.zeros((1, lanes - count), F32)], axis=1)
    weight_col = jnp.sum(jnp.where(taxon_hot, weights, 0.0), axis=1, keepdims=True)
    tnext_s[...] = target_ref[0:edge, :]
    wnext_s[...] = jnp.broadcast_to(weight_col[0:edge], (edge, lanes))
    wait_for = peers - 1 + groups - 1

    def exchange(source, landing, send_sem, recv_sem):
        pltpu.make_async_copy(source.at[me], landing.at[me], recv_sem).start()
        push(source.at[peers], landing.at[peers], send_sem, recv_sem, right, ch).start()

        def body(step, carry):
            to = lax.rem(me + step, peers)
            push(source.at[to], landing.at[me], send_sem, recv_sem, to, ch).start()
            return carry

        lax.fori_loop(1, peers, body, 0)

    def exchange_back(source, landing, send_sem, recv_sem):
        pltpu.make_async_copy(source.at[me], landing.at[me], recv_sem).start()
        push(source.at[peers], landing.at[peers], send_sem, recv_sem, left, ch).start()

        def body(step, carry):
            to = lax.rem(me + step, peers)
            push(source.at[to], landing.at[me], send_sem, recv_sem, to, ch).start()
            return carry

        lax.fori_loop(1, peers, body, 0)

    pack(0, 0)
    pl.semaphore_wait(barrier, wait_for)
    exchange(meta_s, meta_r, sem_ms.at[0], sem_mr.at[0])
    target_push = push(tnext_s, tnext_r, sem_x.at[0], sem_x.at[1], left, ch)
    weight_push = push(wnext_s, wnext_r, sem_x.at[12], sem_x.at[13], left, ch)
    exchange(send_b.at[0], recv_b.at[0], sem_as.at[0], sem_ar.at[0])

    def pack_and_send(c, carry):
        pack(c, 0)
        exchange(send_b.at[c], recv_b.at[c], sem_as.at[c], sem_ar.at[c])
        return carry

    lax.fori_loop(1, chunks, pack_and_send, 0)
    target_push.start()
    weight_push.start()

    short_b[:, 0:short_taps, :] = short_ref[...].astype(F32)

    def filter_spectrum(u, carry):
        cols = pl.ds(pl.multiple_of(u * pair_lanes, pair_lanes), pair_lanes)
        x = filter_ref[:, cols]
        found = jnp.dot(taps_hi[...], x, preferred_element_type=F32) + jnp.dot(
            taps_lo[...], x, preferred_element_type=F32
        )
        spec_b[2 * u] = found[:, :lanes]
        spec_b[2 * u + 1] = found[:, lanes:]
        return carry

    lax.fori_loop(0, col_tiles // 2, filter_spectrum, 0)
    lacc[...] = jnp.zeros_like(lacc)

    drain(meta_r, sem_mr.at[0])
    meta = meta_r[...].reshape(slots, lanes)
    pick = jnp.where(iota((8, lanes), 1) == 0, 1.0, 0.0).astype(BF16)
    found_row = lax.dot_general(
        pick, meta, (((1,), (1,)), ((), ())), preferred_element_type=F32
    )[0:1, :]
    landed_row = found_row + slot_stream_row
    landed_col = meta[:, 0:1].astype(F32) + slot_stream_col
    target_lane = (lane_local + 1).astype(F32) + lane_stream.astype(F32) * stream_step
    place_m[...] = jnp.where(landed_col == target_lane, 1.0, 0.0).astype(BF16)
    own_index = (iota((rows, 1), 0) + 1).astype(F32)
    for s in range(3):
        unpack_m[s * rows : (s + 1) * rows, :] = jnp.where(
            own_index + s * stream_step == landed_row, 1.0, 0.0
        ).astype(BF16)
    target_push.wait()
    weight_push.wait()
    not_first = jnp.where(me > 0, 1.0, 0.0)
    not_last = jnp.where(me < peers - 1, 1.0, 0.0)

    def tile_range(c):
        return pl.ds(c * tiles, tiles)

    def prev_push(c):
        return push(prev_s.at[c], prev_r.at[c], sem_ps.at[c], sem_pr.at[c], right, ch)

    def next_push(c):
        return push(next_s.at[c], next_r.at[c], sem_ns.at[c], sem_nr.at[c], left, ch)

    def gated_push(c):
        return push(
            gext_b.at[tile_range(c), taps_at : taps_at + taps, :],
            gext_b.at[tile_range(c), 0:taps, :],
            sem_gs.at[c],
            sem_gr.at[c],
            right,
            ch,
        )

    taps_at = rows

    def mixed_push(c):
        return push(
            gm_b.at[tile_range(c), 0 : taps + edge, :],
            gm_b.at[tile_range(c), rows : rows + taps + edge, :],
            sem_gs.at[chunks + c],
            sem_gr.at[chunks + c],
            left,
            ch,
        )

    def land(c):
        drain(recv_b.at[c], sem_ar.at[c])

        def body(u, carry):
            local = pl.ds(pl.multiple_of(u * pair_lanes, pair_lanes), pair_lanes)
            got = recv_b[c, :, :, local].reshape(slots, pair_lanes)
            placed = jnp.dot(unpack_m[...], got, preferred_element_type=F32)
            for part in range(2):
                at = c * tiles + 2 * u + part
                piece = placed[:, part * lanes : (part + 1) * lanes]
                for s in range(3):
                    rows_b[s, at, edge : edge + rows, :] = piece[s * rows : (s + 1) * rows]
                    prev_s[c, s, 2 * u + part] = piece[
                        (s + 1) * rows - edge : (s + 1) * rows
                    ].astype(BF16)
                    if s > 0:
                        next_s[c, s - 1, 2 * u + part] = piece[
                            s * rows : s * rows + edge
                        ].astype(BF16)
            return carry

        lax.fori_loop(0, pairs, body, 0)
        prev_push(c).start()
        next_push(c).start()

    def convolve(c):
        prev_push(c).wait()
        next_push(c).wait()

        def body(u, carry):
            at = c * tiles + u
            cols = pl.ds(pl.multiple_of(at * lanes, lanes), lanes)
            for s in range(3):
                rows_b[s, at, 0:edge, :] = prev_r[c, s, u].astype(F32) * not_first
            for s in range(2):
                rows_b[s + 1, at, edge + rows : 2 * edge + rows, :] = next_r[c, s, u].astype(F32)

            def conv(s, total):
                summed = None
                for j in range(short_taps):
                    term = (
                        short_b[s, j : j + 1, cols]
                        * rows_b[s, at, edge - j : edge - j + total, :]
                    )
                    summed = term if summed is None else summed + term
                return summed

            k_conv = conv(1, ext)
            v_conv = conv(2, ext)
            kc_b[at] = k_conv
            vc_b[at] = v_conv
            gext_b[at, taps : taps + ext, :] = (k_conv * v_conv).astype(BF16)
            q_conv = conv(0, rows)
            qc_b[at] = q_conv
            out_grad = weight_col[0:rows] * target_ref[:, cols].astype(F32)
            go_b[at, 0:rows, :] = out_grad
            go_b[at, rows:ext, :] = (
                wnext_r[...] * tnext_r[:, cols].astype(F32) * not_last
            )
            gm_b[at, 0:rows, :] = (out_grad * q_conv).astype(BF16)
            return carry

        lax.fori_loop(0, tiles, body, 0)
        gated_push(c).start()
        mixed_push(c).start()

    def both(high, low, x):
        return jnp.dot(high, x, preferred_element_type=F32) + jnp.dot(
            low, x, preferred_element_type=F32
        )

    def inverse(high, low, real, imag):
        y = jnp.concatenate([real, imag], axis=0)
        y_hi = y.astype(BF16)
        y_lo = (y - y_hi.astype(F32)).astype(BF16)
        return both(high[...], low[...], y_hi) + jnp.dot(
            high[...], y_lo, preferred_element_type=F32
        )

    def backward(c):
        gated_push(c).wait()
        mixed_push(c).wait()

        @pl.when(me == 0)
        def _():
            def clear(u, carry):
                gext_b[c * tiles + u, 0:taps, :] = jnp.zeros((taps, lanes), BF16)
                return carry

            lax.fori_loop(0, tiles, clear, 0)

        @pl.when(me == peers - 1)
        def _():
            def clear(u, carry):
                gm_b[c * tiles + u, rows : rows + taps + edge, :] = jnp.zeros(
                    (taps + edge, lanes), BF16
                )
                return carry

            lax.fori_loop(0, tiles, clear, 0)

        def body(u, carry):
            first = c * tiles + 2 * u
            gx = jnp.concatenate([gext_b[first], gext_b[first + 1]], axis=1)
            g_own = jnp.concatenate(
                [gm_b[first, 0:rows, :], gm_b[first + 1, 0:rows, :]], axis=1
            )
            g_later = jnp.concatenate(
                [
                    gm_b[first, rows : rows + taps + edge, :],
                    gm_b[first + 1, rows : rows + taps + edge, :],
                ],
                axis=1,
            )
            spec = jnp.concatenate([spec_b[first], spec_b[first + 1]], axis=1)
            fr, fi = spec[:rows], spec[rows:]
            sg = both(ahead_hi[...], ahead_lo[...], gx)
            gr, gi = sg[:rows], sg[rows:]
            mixed = inverse(mixed_hi, mixed_lo, fr * gr - fi * gi, fr * gi + fi * gr)
            so = both(own_hi[...], own_lo[...], g_own)
            mr, mi = so[:rows], so[rows:]
            taps_grad = inverse(filter_hi, filter_lo, mr * gr + mi * gi, mr * gi - mi * gr)
            sl = both(later_hi[...], later_lo[...], g_later)
            ar, ai = mr + sl[:rows], mi + sl[rows:]
            gated_grad = inverse(gated_hi, gated_lo, fr * ar + fi * ai, fr * ai - fi * ar)
            for part in range(2):
                at = first + part
                cols = pl.ds(pl.multiple_of(at * lanes, lanes), lanes)
                lane_cut = slice(part * lanes, (part + 1) * lanes)
                mix = mixed[:, lane_cut]
                gg = gated_grad[:, lane_cut]
                par_b[at, 0:taps, :] = taps_grad[:, lane_cut] * grad_scale
                par_b[at, payload - 32 : payload, :] = jnp.zeros((32, lanes), F32)
                out = (qc_b[at] * mix[:rows]).astype(BF16)
                out_ref[:, cols] = out
                lacc[...] += out.astype(F32) * target_ref[:, cols].astype(F32)
                gbuf[0] = go_b[at] * mix
                gbuf[1] = gg * vc_b[at]
                gbuf[2] = gg * kc_b[at]
                for s in range(3):
                    own = gbuf[s, 0:rows, :]
                    back = None
                    for j in range(short_taps):
                        found = jnp.sum(
                            own * rows_b[s, at, edge - j : edge - j + rows, :],
                            axis=0,
                            keepdims=True,
                        )
                        par_b[at, taps + s * short_taps + j : taps + s * short_taps + j + 1, :] = (
                            found * grad_scale
                        )
                        term = short_b[s, j : j + 1, cols] * gbuf[s, j : j + rows, :]
                        back = term if back is None else back + term
                    gr_b[s * rows : (s + 1) * rows, lane_cut] = back.astype(BF16)
            local = pl.ds(pl.multiple_of(u * pair_lanes, pair_lanes), pair_lanes)
            packed = jnp.dot(place_m[...], gr_b[...], preferred_element_type=F32).astype(BF16)
            bsend_b[c, :, :, local] = packed.reshape(blocks, block_rows, pair_lanes)
            return carry

        lax.fori_loop(0, pairs, body, 0)
        exchange_back(bsend_b.at[c], brecv_b.at[c], sem_bs.at[c], sem_br.at[c])

    def steps(t, carry):
        @pl.when(jnp.logical_and(t >= 2, t < chunks + 2))
        def _():
            backward(t - 2)

        @pl.when(jnp.logical_and(t >= 1, t < chunks + 1))
        def _():
            convolve(t - 1)

        @pl.when(t < chunks)
        def _():
            land(t)

        return carry

    lax.fori_loop(0, chunks + 2, steps, 0)

    row_loss = jnp.sum(lacc[...], axis=1, keepdims=True)
    taxon_part = (
        jnp.sum(jnp.where(taxon_hot[0:rows], row_loss, 0.0), axis=0, keepdims=True) * loss_scale
    )
    lch_s[...] = jnp.broadcast_to(taxon_part, (8, lanes))
    lch_r[ch] = jnp.broadcast_to(taxon_part, (8, lanes))

    def loss_push(step):
        return push(
            lch_s, lch_r.at[ch], sem_x.at[8 + step], sem_x.at[2], me, lax.rem(ch + step, groups)
        )

    for step in range(1, groups):
        loss_push(step).start()

    def fill(j, carry):
        rs_s[2 * j] = par_b[j, 0:half_rows, :].astype(BF16)
        rs_s[2 * j + 1] = par_b[j, half_rows:payload, :].astype(BF16)
        return carry

    lax.fori_loop(0, col_tiles, fill, 0)

    def scatter(step, carry):
        to = lax.rem(me + step, peers)
        push(rs_s.at[to], rs_r.at[me], sem_x.at[3], sem_x.at[4], to, ch).start()
        return carry

    pltpu.make_async_copy(rs_s.at[me], rs_r.at[me], sem_x.at[4]).start()
    lax.fori_loop(1, peers, scatter, 0)

    def finish(c, carry):
        drain(brecv_b.at[c], sem_br.at[c])

        def body(u, inner):
            local = pl.ds(pl.multiple_of(u * pair_lanes, pair_lanes), pair_lanes)
            cols = pl.ds(pl.multiple_of(c * width + u * pair_lanes, pair_lanes), pair_lanes)
            got = brecv_b[c, :, :, local].reshape(slots, pair_lanes)
            back = jnp.dot(return_m[...], got, preferred_element_type=F32).astype(BF16)
            qg_ref[:, cols] = back[0:rows]
            kg_ref[:, cols] = back[rows : 2 * rows]
            vg_ref[:, cols] = back[2 * rows : 3 * rows]
            return inner

        lax.fori_loop(0, pairs, body, 0)
        return carry

    lax.fori_loop(0, chunks - 1, finish, 0)

    if groups > 1:
        drain(lch_r.at[0 : groups - 1], sem_x.at[2])
    total = lch_r[0]
    for g in range(1, groups):
        total = total + lch_r[g]
    lct_s[...] = total
    lct_r[me] = total

    def share_loss(step, carry):
        to = lax.rem(me + step, peers)
        push(lct_s, lct_r.at[me], sem_x.at[5], sem_x.at[6], to, ch).start()
        return carry

    lax.fori_loop(1, peers, share_loss, 0)

    drain(rs_r, sem_x.at[4])

    def add(j, summed):
        return summed + rs_r[j].astype(F32)

    ag_s[...] = lax.fori_loop(1, peers, add, rs_r[0].astype(F32)).astype(BF16)

    def gather(step, carry):
        to = lax.rem(me + step, peers)
        push(ag_s, ag_r.at[me], sem_x.at[7], sem_x.at[8], to, ch).start()
        return carry

    pltpu.make_async_copy(ag_s, ag_r.at[me], sem_x.at[8]).start()
    lax.fori_loop(1, peers, gather, 0)

    finish(chunks - 1, 0)
    drain(lct_r.at[0 : peers - 1], sem_x.at[6])

    def add_loss(j, summed):
        return summed + lct_r[j]

    loss_ref[...] = lax.fori_loop(1, peers, add_loss, lct_r[0])
    drain(ag_r, sem_x.at[8])

    def emit(j, carry):
        cols = pl.ds(pl.multiple_of(j * lanes, lanes), lanes)
        par_b[j, 0:half_rows, :] = ag_r[2 * j].astype(F32)
        par_b[j, half_rows:payload, :] = ag_r[2 * j + 1].astype(F32)
        fg_ref[:, cols] = par_b[j, 0:taps, :]
        for s in range(3):
            sg_ref[s, :, cols] = par_b[
                j, taps + s * short_taps : taps + (s + 1) * short_taps, :
            ]
        return carry

    lax.fori_loop(0, col_tiles, emit, 0)

    drain(meta_s.at[0:peers], sem_ms.at[0])
    for step in range(1, groups):
        loss_push(step).wait_send()
    drain(rs_s.at[0 : peers - 1], sem_x.at[3])
    drain(lct_r.at[0 : peers - 1], sem_x.at[5])
    drain(ag_r.at[0 : peers - 1], sem_x.at[7])

    def sent(c, carry):
        drain(send_b.at[c, 0:peers], sem_as.at[c])
        drain(bsend_b.at[c, 0:peers], sem_bs.at[c])
        return carry

    lax.fori_loop(0, chunks, sent, 0)


def shards(
    query_in,
    key_in,
    value_in,
    row_place,
    short_weight,
    long_filter,
    target,
    taxon_ids,
    taxon_weight,
):
    rows, channels = query_in.shape
    peers = lax.axis_size("ctx")
    groups = lax.axis_size("ch")
    taps = long_filter.shape[0]
    short_taps = short_weight.shape[1]
    width = channels // chunks
    col_tiles = channels // lanes
    tiles = width // lanes
    blocks = peers + 1
    slots = blocks * block_rows
    ext = rows + edge
    span = taps + ext
    payload = payload_rows(taps, short_taps)
    half_rows = payload // 2
    tables = []
    made = dft_tables(rows, taps)
    for name in table_names:
        high, low = split_constant(made[name])
        tables.append(jnp.asarray(high))
        tables.append(jnp.asarray(low))
    vm = pltpu.VMEM
    dma = pltpu.SemaphoreType.DMA
    shape = jax.ShapeDtypeStruct
    scratch = [
        vm((slots, 3 * rows), BF16),
        vm((3 * rows, slots), BF16),
        vm((slots, 3 * rows), BF16),
        vm((3 * rows, slots), BF16),
        vm((chunks, blocks, block_rows, width), BF16),
        vm((chunks, blocks, block_rows, width), BF16),
        vm((blocks, block_rows, lanes), BF16),
        vm((blocks, block_rows, lanes), BF16),
        vm((chunks, blocks, block_rows, width), BF16),
        vm((chunks, blocks, block_rows, width), BF16),
        vm((3, col_tiles, rows + 2 * edge, lanes), F32),
        vm((chunks, 3, tiles, edge, lanes), BF16),
        vm((chunks, 3, tiles, edge, lanes), BF16),
        vm((chunks, 2, tiles, edge, lanes), BF16),
        vm((chunks, 2, tiles, edge, lanes), BF16),
        vm((edge, channels), BF16),
        vm((edge, channels), BF16),
        vm((edge, lanes), F32),
        vm((edge, lanes), F32),
        vm((col_tiles, rows, lanes), F32),
        vm((col_tiles, ext, lanes), F32),
        vm((col_tiles, ext, lanes), F32),
        vm((col_tiles, ext, lanes), F32),
        vm((col_tiles, span, lanes), BF16),
        vm((col_tiles, span, lanes), BF16),
        vm((col_tiles, 2 * rows, lanes), F32),
        vm((3, 8, channels), F32),
        vm((3, ext, lanes), F32),
        vm((3 * rows, 2 * lanes), BF16),
        vm((rows, lanes), F32),
        vm((col_tiles, payload, lanes), F32),
        vm((2 * col_tiles, half_rows, lanes), BF16),
        vm((peers, half_rows, lanes), BF16),
        vm((half_rows, lanes), BF16),
        vm((peers, half_rows, lanes), BF16),
        vm((8, lanes), F32),
        vm((groups, 8, lanes), F32),
        vm((8, lanes), F32),
        vm((peers, 8, lanes), F32),
        dma((chunks,)),
        dma((chunks,)),
        dma((chunks,)),
        dma((chunks,)),
        dma((chunks,)),
        dma((chunks,)),
        dma((chunks,)),
        dma((chunks,)),
        dma((2 * chunks,)),
        dma((2 * chunks,)),
        dma((1,)),
        dma((1,)),
        dma((16,)),
    ]
    inputs = (
        query_in,
        key_in,
        value_in,
        row_place.reshape(1, rows),
        jnp.tile(row_place, 3).reshape(1, 3 * rows),
        short_weight,
        long_filter,
        target,
        taxon_ids.reshape(1, rows),
        taxon_weight.reshape(1, -1),
        *tables,
    )
    gated_out, query_grad, key_grad, value_grad, filter_grad, short_grad, losses = pl.pallas_call(
        lambda *refs: whole_kernel(peers, groups, *refs),
        out_shape=(
            shape((rows, channels), BF16),
            shape((rows, channels), BF16),
            shape((rows, channels), BF16),
            shape((rows, channels), BF16),
            shape((taps, channels), F32),
            shape((3, short_taps, channels), F32),
            shape((8, lanes), F32),
        ),
        in_specs=[pl.BlockSpec(memory_space=pltpu.VMEM)] * len(inputs),
        out_specs=[pl.BlockSpec(memory_space=pltpu.VMEM)] * 7,
        scratch_shapes=scratch,
        compiler_params=pltpu.CompilerParams(
            collective_id=0, has_side_effects=True, vmem_limit_bytes=63_000_000
        ),
        name="hyena",
    )(*inputs)
    return (
        gated_out,
        query_grad,
        key_grad,
        value_grad,
        filter_grad,
        short_grad,
        losses[0, : taxon_weight.shape[0]],
    )


def solution(mesh):
    placed = (
        P("ctx", "ch"),
        P("ctx", "ch"),
        P("ctx", "ch"),
        P("ctx"),
        P(None, None, "ch"),
        P(None, "ch"),
        P("ctx", "ch"),
        P("ctx"),
        P(),
    )
    return jax.shard_map(
        shards,
        mesh=mesh,
        in_specs=placed,
        out_specs=(
            P("ctx", "ch"),
            P("ctx", "ch"),
            P("ctx", "ch"),
            P("ctx", "ch"),
            P(None, "ch"),
            P(None, None, "ch"),
            P(),
        ),
        check_vma=False,
    )
```

time: 800 us -> 130 us (0.16); the launches traced: 787 us -> 130 us
  local copies, waits for them, and re-layouts: 398 us -> 9.37 us
  Pallas kernels: 0 us -> 120 us
  waiting for transfers between devices: 110 us -> 0 us
  starting transfers between devices: 73.4 us -> 0 us
  matrix products: 67.7 us -> 0 us
  blocking collectives: 67.3 us -> 0 us
  other arithmetic: 55 us -> 0 us
  between operations: 15.5 us -> 0.66 us
    reshape x18 -> x0, local copies, waits for them, and re-layouts: 173 us -> none  [the longest x2 95.6 us: skew_rows(): return picked.reshape(tile_rows, span_width, channels)]
    pallas_call x0 -> x1, Pallas kernels: none -> 120 us  [shards(): pl.pallas_call(lambda *refs: whole_kernel(peers, groups, *refs), out_shap...]
    all_to_all x7 -> x0, waiting for transfers between devices: 83.3 us -> none  [the longest x1 25.3 us: shards(): lax.all_to_all(pack_rows(key_in), 'ctx', split_axis=0, concat_axis=0, til...]
    gather x14 -> x0, local copies, waits for them, and re-layouts: 78.8 us -> none  [the longest x2 51.7 us: skew_rows(): jnp.take(row, jnp.asarray(table.reshape(-1), dtype=jnp.int32), axis=0)]
    transpose x3 -> x0, local copies, waits for them, and re-layouts: 71.9 us -> none  [the longest x1 61.3 us: shards(): jnp.einsum('nac,nbc->abc', grad_mixed.reshape(-1, tile_rows, channels), w...]
    dot_general x5 -> x0, matrix products: 67.7 us -> none  [the longest x1 27.7 us: shards(): jnp.einsum('nac,nbc->abc', grad_mixed.reshape(-1, tile_rows, channels), w...]
    psum x1 -> x0, blocking collectives: 67.3 us -> none  [shards(): taxon_loss = lax.psum(loss_part, ('ctx', 'ch'))]
    all_to_all x7 -> x0, starting transfers between devices: 54.2 us -> none  [the longest x1 11.8 us: shards(): lax.all_to_all(return_rows(grad_value).reshape(peer_count, capacity, chan...]
  transfers between devices with their start and end apart: 16 -> 0, of which waited for: 7 -> 0; matrix products, arithmetic and copies ran while one was open for 61% -> 0% of each run, Pallas kernels for 0% -> 0%
where the time goes in v1:
time: 130 us
  Pallas kernels  120 us (92%)
  local copies, waits for them, and re-layouts  9.37 us (7%)
    pallas_call x1, Pallas kernels, shards(): pl.pallas_call(lambda *refs: whole_kernel(peers, groups, *refs), out_shap...  120 us
    unnamed x18, local copies, waits for them, and re-layouts  7.52 us

profile of v1, /device:TPU:1, one launch (start us, length us, event | category | flops | bytes accessed | tf_op | source)
XLA Modules:
  0.0 130.2 jit_solution(12305781317182572545)
XLA Ops:
  0.6 0.0 copy-start.5
  0.6 0.7 copy-done.5
  1.3 0.7 reshape_tile.3.refs_4_
  2.0 120.1 %hyena.1 = (bf16[160,2048]{1,0:T(8,128)(2,1)}, bf16[160,2048]{1,0:T(8,128)(2,1)}, bf16[160,2048]{1,0:T(8,128)(2,1)}, bf16[160,2048]{1,0:T(8,128)(2,1)}, f32[128,...) custom-call(bf16[160,2048]{1,0:T(8,128)(2,1)} %refs_0_.1, bf16[160,2048]{1,0:T(8,128)(2,1)} %refs_1_.1, ...), custom_call_target="tpu_custom_call" | custom-call | tf_op jit(solution)/shard_map/hyena/pallas_call | solution.py:791
  122.1 1.2 slice_bitcast_fusion
  123.3 0.0 copy-start.3
  123.3 2.0 %copy.36 = bf16[160,2048]{1,0:T(8,128)(2,1)} copy(bf16[160,2048]{1,0:T(8,128)(2,1)} %get-tuple-element.28) | data formatting | bytes 1310720
  125.4 0.0 copy-done.3
  125.4 0.0 copy-start.2
  125.4 0.0 copy-start.1
  125.4 0.8 copy.37
  126.2 0.5 copy-done.2
  126.7 0.0 copy-start
  126.7 0.8 copy.38
  127.5 0.0 copy-done.1
  127.5 0.8 copy.39
  128.4 0.0 copy-done
  128.4 0.0 copy-start.4
  128.4 1.0 copy.40
  129.3 0.1 copy-done.4
  129.5 0.7 copy.41
  (1 shorter events, 0.0 us)
Async XLA Ops:
  0.6 0.7 copy-start.5
  123.3 2.1 %copy-start.3 = (bf16[160,2048]{1,0:T(8,128)(2,1)S(1)}, bf16[160,2048]{1,0:T(8,128)(2,1)}, u32[]{:S(2)}) copy-start(bf16[160,2048]{1,0:T(8,128)(2,1)} %get-tuple-element.29) | copy-start | bytes 1966084
  125.4 1.3 %copy-start.2 = (bf16[160,2048]{1,0:T(8,128)(2,1)S(1)}, bf16[160,2048]{1,0:T(8,128)(2,1)}, u32[]{:S(2)}) copy-start(bf16[160,2048]{1,0:T(8,128)(2,1)} %get-tuple-element.30) | copy-start | bytes 1966084
  125.4 2.2 %copy-start.1 = (bf16[160,2048]{1,0:T(8,128)(2,1)S(1)}, bf16[160,2048]{1,0:T(8,128)(2,1)}, u32[]{:S(2)}) copy-start(bf16[160,2048]{1,0:T(8,128)(2,1)} %get-tuple-element.31) | copy-start | bytes 1966084
  126.7 1.7 %copy-start = (f32[128,2048]{1,0:T(8,128)S(1)}, f32[128,2048]{1,0:T(8,128)}, u32[]{:S(2)}) copy-start(f32[128,2048]{1,0:T(8,128)} %get-tuple-element.32) | copy-start | bytes 3145732
  128.4 1.1 copy-start.4

commit v2 on v1

--- a/solution.py
+++ b/solution.py
@@ -51,7 +51,7 @@
     return tables
 
 
-table_names = ("ahead", "own", "later", "taps", "mixed", "gated", "filter")
+table_names = ("taps", "ahead", "own", "later", "mixed", "gated", "filter")
 
 
 def payload_rows(taps, short_taps):
@@ -74,90 +74,93 @@
 def whole_kernel(
     peers,
     groups,
-    q_ref,
-    k_ref,
-    v_ref,
     place_ref,
-    place3_ref,
-    short_ref,
-    filter_ref,
-    target_ref,
     taxon_ref,
     weight_ref,
-    ahead_hi,
-    ahead_lo,
-    own_hi,
-    own_lo,
-    later_hi,
-    later_lo,
-    taps_hi,
-    taps_lo,
-    mixed_hi,
-    mixed_lo,
-    gated_hi,
-    gated_lo,
-    filter_hi,
-    filter_lo,
-    out_ref,
-    qg_ref,
-    kg_ref,
-    vg_ref,
-    fg_ref,
-    sg_ref,
-    loss_ref,
-    pack_m,
-    unpack_m,
-    place_m,
-    return_m,
-    send_b,
-    recv_b,
-    meta_s,
-    meta_r,
-    bsend_b,
-    brecv_b,
-    rows_b,
-    prev_s,
-    prev_r,
-    next_s,
-    next_r,
-    tnext_s,
-    tnext_r,
-    wnext_s,
-    wnext_r,
-    qc_b,
-    kc_b,
-    vc_b,
-    go_b,
-    gext_b,
-    gm_b,
-    spec_b,
-    short_b,
-    gbuf,
-    gr_b,
-    lacc,
-    par_b,
-    rs_s,
-    rs_r,
-    ag_s,
-    ag_r,
-    lch_s,
-    lch_r,
-    lct_s,
-    lct_r,
-    sem_as,
-    sem_ar,
-    sem_bs,
-    sem_br,
-    sem_ps,
-    sem_pr,
-    sem_ns,
-    sem_nr,
-    sem_gs,
-    sem_gr,
-    sem_ms,
-    sem_mr,
-    sem_x,
+    short_ref,
+    *refs,
 ):
+    far = refs[:19]
+    out_hbm, brecv_b, return_hbm, ag_r, loss_ref = refs[19:24]
+    near = refs[24:43]
+    (
+        q_ref,
+        k_ref,
+        v_ref,
+        target_ref,
+        filter_ref,
+        taps_hi,
+        taps_lo,
+        ahead_hi,
+        ahead_lo,
+        own_hi,
+        own_lo,
+        later_hi,
+        later_lo,
+        mixed_hi,
+        mixed_lo,
+        gated_hi,
+        gated_lo,
+        filter_hi,
+        filter_lo,
+    ) = near
+    sem_in = refs[43]
+    (
+        out_ref,
+        pack_m,
+        unpack_m,
+        place_m,
+        return_m,
+        send_b,
+        recv_b,
+        meta_s,
+        meta_r,
+        bsend_b,
+        rows_b,
+        prev_s,
+        prev_r,
+        next_s,
+        next_r,
+        tnext_s,
+        tnext_r,
+        wnext_s,
+        wnext_r,
+        qc_b,
+        kc_b,
+        vc_b,
+        go_b,
+        gext_b,
+        gm_b,
+        spec_b,
+        short_b,
+        gbuf,
+        gr_b,
+        lacc,
+        par_b,
+        rs_s,
+        rs_r,
+        ag_s,
+        lch_s,
+        lch_r,
+        lct_s,
+        lct_r,
+        sem_as,
+        sem_ar,
+        sem_bs,
+        sem_br,
+        sem_ps,
+        sem_pr,
+        sem_ns,
+        sem_nr,
+        sem_gs,
+        sem_gr,
+        sem_ms,
+        sem_mr,
+        sem_rs,
+        sem_rr,
+        sem_out,
+        sem_x,
+    ) = refs[44:]
     rows, channels = q_ref.shape
     taps = filter_ref.shape[0]
     short_taps = short_ref.shape[1]
@@ -169,6 +172,7 @@
     slots = blocks * block_rows
     ext = rows + edge
     payload = payload_rows(taps, short_taps)
+    share = peers // chunks
     half_rows = payload // 2
     me = lax.axis_index("ctx")
     ch = lax.axis_index("ch")
@@ -190,6 +194,12 @@
         pl.semaphore_signal(
             barrier, inc=1, device_id=(me, lax.rem(ch + step, groups)), device_id_type=MESH
         )
+
+    def fetch(index):
+        return pltpu.make_async_copy(far[index], near[index], sem_in.at[index])
+
+    for index in range(len(far)):
+        fetch(index).start()
 
     def push(src, dst, send_sem, recv_sem, ctx_to, ch_to):
         return pltpu.make_async_remote_copy(
@@ -209,7 +219,7 @@
         return jnp.sum(jnp.where(eye, row_vector, 0.0), axis=1, keepdims=True)
 
     place_row = place_ref[...].astype(F32)
-    place3_row = place3_ref[...].astype(F32)
+    place3_row = jnp.concatenate([place_row] * 3, axis=1)
     owner_row = jnp.floor((place_row + 0.5) * (1.0 / rows))
     owner3_row = jnp.floor((place3_row + 0.5) * (1.0 / rows))
     owner_col = column(owner_row, rows)
@@ -251,11 +261,6 @@
     slot_key_row, slot_stream_row = static_key((1, slots), 1)
     full3_row = key3_row + lane_stream.astype(F32) * stream_step
     pack_m[...] = jnp.where(slot_key_col == full3_row, 1.0, 0.0).astype(BF16)
-    for s in range(3):
-        return_m[s * rows : (s + 1) * rows, :] = jnp.where(
-            key_col + s * stream_step == slot_key_row, 1.0, 0.0
-        ).astype(BF16)
-
     meta_col = jnp.broadcast_to(local_col + 1.0, (rows, lanes)).astype(BF16)
     meta3 = jnp.concatenate([meta_col] * 3, axis=0)
     meta_s[...] = (
@@ -279,6 +284,46 @@
         lax.fori_loop(0, pairs, body, 0)
         return carry
 
+    wait_for = peers - 1 + groups - 1
+
+    def exchange(source, landing, send_sem, recv_sem):
+        pltpu.make_async_copy(source.at[me], landing.at[me], recv_sem).start()
+        push(source.at[peers], landing.at[peers], send_sem, recv_sem, right, ch).start()
+
+        def body(step, carry):
+            to = lax.rem(me + step, peers)
+            push(source.at[to], landing.at[me], send_sem, recv_sem, to, ch).start()
+            return carry
+
+        lax.fori_loop(1, peers, body, 0)
+
+    def exchange_back(source, landing, send_sem, recv_sem):
+        pltpu.make_async_copy(source.at[me], landing.at[me], recv_sem).start()
+        push(source.at[peers], landing.at[peers], send_sem, recv_sem, left, ch).start()
+
+        def body(step, carry):
+            to = lax.rem(me + step, peers)
+            push(source.at[to], landing.at[me], send_sem, recv_sem, to, ch).start()
+            return carry
+
+        lax.fori_loop(1, peers, body, 0)
+
+    for index in range(3):
+        fetch(index).wait()
+    pack(0, 0)
+    pl.semaphore_wait(barrier, wait_for)
+    exchange(meta_s, meta_r, sem_ms.at[0], sem_mr.at[0])
+    target_push = push(tnext_s, tnext_r, sem_x.at[0], sem_x.at[1], left, ch)
+    weight_push = push(wnext_s, wnext_r, sem_x.at[12], sem_x.at[13], left, ch)
+    exchange(send_b.at[0], recv_b.at[0], sem_as.at[0], sem_ar.at[0])
+
+    def pack_and_send(c, carry):
+        pack(c, 0)
+        exchange(send_b.at[c], recv_b.at[c], sem_as.at[c], sem_ar.at[c])
+        return carry
+
+    lax.fori_loop(1, chunks, pack_and_send, 0)
+    fetch(3).wait()
     ids_row = taxon_ref[...].astype(F32)
     ids_col = column(ids_row, rows)
     count = weight_ref.shape[1]
@@ -287,45 +332,17 @@
     weight_col = jnp.sum(jnp.where(taxon_hot, weights, 0.0), axis=1, keepdims=True)
     tnext_s[...] = target_ref[0:edge, :]
     wnext_s[...] = jnp.broadcast_to(weight_col[0:edge], (edge, lanes))
-    wait_for = peers - 1 + groups - 1
-
-    def exchange(source, landing, send_sem, recv_sem):
-        pltpu.make_async_copy(source.at[me], landing.at[me], recv_sem).start()
-        push(source.at[peers], landing.at[peers], send_sem, recv_sem, right, ch).start()
-
-        def body(step, carry):
-            to = lax.rem(me + step, peers)
-            push(source.at[to], landing.at[me], send_sem, recv_sem, to, ch).start()
-            return carry
-
-        lax.fori_loop(1, peers, body, 0)
-
-    def exchange_back(source, landing, send_sem, recv_sem):
-        pltpu.make_async_copy(source.at[me], landing.at[me], recv_sem).start()
-        push(source.at[peers], landing.at[peers], send_sem, recv_sem, left, ch).start()
-
-        def body(step, carry):
-            to = lax.rem(me + step, peers)
-            push(source.at[to], landing.at[me], send_sem, recv_sem, to, ch).start()
-            return carry
-
-        lax.fori_loop(1, peers, body, 0)
-
-    pack(0, 0)
-    pl.semaphore_wait(barrier, wait_for)
-    exchange(meta_s, meta_r, sem_ms.at[0], sem_mr.at[0])
-    target_push = push(tnext_s, tnext_r, sem_x.at[0], sem_x.at[1], left, ch)
-    weight_push = push(wnext_s, wnext_r, sem_x.at[12], sem_x.at[13], left, ch)
-    exchange(send_b.at[0], recv_b.at[0], sem_as.at[0], sem_ar.at[0])
-
-    def pack_and_send(c, carry):
-        pack(c, 0)
-        exchange(send_b.at[c], recv_b.at[c], sem_as.at[c], sem_ar.at[c])
-        return carry
-
-    lax.fori_loop(1, chunks, pack_and_send, 0)
     target_push.start()
     weight_push.start()
+    for s in range(3):
+        return_m[s * rows : (s + 1) * rows, :] = jnp.where(
+            key_col + s * stream_step == slot_key_row, 1.0, 0.0
+        ).astype(BF16)
+
+    return_copy = pltpu.make_async_copy(return_m, return_hbm, sem_x.at[14])
+    return_copy.start()
+    for index in range(4, len(far)):
+        fetch(index).wait()
 
     short_b[:, 0:short_taps, :] = short_ref[...].astype(F32)
 
@@ -341,6 +358,7 @@
 
     lax.fori_loop(0, col_tiles // 2, filter_spectrum, 0)
     lacc[...] = jnp.zeros_like(lacc)
+    par_b[...] = jnp.zeros_like(par_b)
 
     drain(meta_r, sem_mr.at[0])
     meta = meta_r[...].reshape(slots, lanes)
@@ -524,8 +542,9 @@
                 lane_cut = slice(part * lanes, (part + 1) * lanes)
                 mix = mixed[:, lane_cut]
                 gg = gated_grad[:, lane_cut]
-                par_b[at, 0:taps, :] = taps_grad[:, lane_cut] * grad_scale
-                par_b[at, payload - 32 : payload, :] = jnp.zeros((32, lanes), F32)
+                found_taps = taps_grad[:, lane_cut].astype(BF16)
+                rs_s[2 * at] = found_taps[0:half_rows]
+                rs_s[2 * at + 1, 0 : taps - half_rows, :] = found_taps[half_rows:]
                 out = (qc_b[at] * mix[:rows]).astype(BF16)
                 out_ref[:, cols] = out
                 lacc[...] += out.astype(F32) * target_ref[:, cols].astype(F32)
@@ -541,32 +560,74 @@
                             axis=0,
                             keepdims=True,
                         )
-                        par_b[at, taps + s * short_taps + j : taps + s * short_taps + j + 1, :] = (
-                            found * grad_scale
-                        )
+                        par_b[s * short_taps + j : s * short_taps + j + 1, :] = found
                         term = short_b[s, j : j + 1, cols] * gbuf[s, j : j + rows, :]
                         back = term if back is None else back + term
                     gr_b[s * rows : (s + 1) * rows, lane_cut] = back.astype(BF16)
+                rs_s[2 * at + 1, taps - half_rows : half_rows, :] = par_b[...].astype(BF16)
             local = pl.ds(pl.multiple_of(u * pair_lanes, pair_lanes), pair_lanes)
             packed = jnp.dot(place_m[...], gr_b[...], preferred_element_type=F32).astype(BF16)
             bsend_b[c, :, :, local] = packed.reshape(blocks, block_rows, pair_lanes)
             return carry
 
         lax.fori_loop(0, pairs, body, 0)
+        out_copy(c).start()
+
+        def scatter(i, carry):
+            piece = c * share + i
+
+            @pl.when(piece == me)
+            def _():
+                pltpu.make_async_copy(rs_s.at[piece], rs_r.at[me], sem_rr.at[0]).start()
+
+            @pl.when(piece != me)
+            def _():
+                push(rs_s.at[piece], rs_r.at[me], sem_rs.at[0], sem_rr.at[0], piece, ch).start()
+
+            return carry
+
+        lax.fori_loop(0, share, scatter, 0)
         exchange_back(bsend_b.at[c], brecv_b.at[c], sem_bs.at[c], sem_br.at[c])
 
+    def reduce(c):
+        @pl.when(me // share == c)
+        def _():
+            drain(rs_r, sem_rr.at[0])
+
+            def add(j, summed):
+                return summed + rs_r[j].astype(F32)
+
+            summed = lax.fori_loop(1, peers, add, rs_r[0].astype(F32))
+            ag_s[...] = (summed * grad_scale).astype(BF16)
+
+            def gather(step, carry):
+                to = lax.rem(me + step, peers)
+                push(ag_s, ag_r.at[me], sem_rs.at[1], sem_rr.at[1], to, ch).start()
+                return carry
+
+            pltpu.make_async_copy(ag_s, ag_r.at[me], sem_rr.at[1]).start()
+            lax.fori_loop(1, peers, gather, 0)
+
+    def out_copy(c):
+        cols = pl.ds(pl.multiple_of(c * width, width), width)
+        return pltpu.make_async_copy(out_ref.at[:, cols], out_hbm.at[:, cols], sem_out.at[c])
+
     def steps(t, carry):
-        @pl.when(jnp.logical_and(t >= 2, t < chunks + 2))
+        @pl.when(t < chunks)
         def _():
-            backward(t - 2)
+            land(t)
 
         @pl.when(jnp.logical_and(t >= 1, t < chunks + 1))
         def _():
             convolve(t - 1)
 
-        @pl.when(t < chunks)
+        @pl.when(t >= 2)
         def _():
-            land(t)
+            backward(t - 2)
+
+        @pl.when(t >= 3)
+        def _():
+            reduce(t - 3)
 
         return carry
 
@@ -586,39 +647,6 @@
 
     for step in range(1, groups):
         loss_push(step).start()
-
-    def fill(j, carry):
-        rs_s[2 * j] = par_b[j, 0:half_rows, :].astype(BF16)
-        rs_s[2 * j + 1] = par_b[j, half_rows:payload, :].astype(BF16)
-        return carry
-
-    lax.fori_loop(0, col_tiles, fill, 0)
-
-    def scatter(step, carry):
-        to = lax.rem(me + step, peers)
-        push(rs_s.at[to], rs_r.at[me], sem_x.at[3], sem_x.at[4], to, ch).start()
-        return carry
-
-    pltpu.make_async_copy(rs_s.at[me], rs_r.at[me], sem_x.at[4]).start()
-    lax.fori_loop(1, peers, scatter, 0)
-
-    def finish(c, carry):
-        drain(brecv_b.at[c], sem_br.at[c])
-
-        def body(u, inner):
-            local = pl.ds(pl.multiple_of(u * pair_lanes, pair_lanes), pair_lanes)
-            cols = pl.ds(pl.multiple_of(c * width + u * pair_lanes, pair_lanes), pair_lanes)
-            got = brecv_b[c, :, :, local].reshape(slots, pair_lanes)
-            back = jnp.dot(return_m[...], got, preferred_element_type=F32).astype(BF16)
-            qg_ref[:, cols] = back[0:rows]
-            kg_ref[:, cols] = back[rows : 2 * rows]
-            vg_ref[:, cols] = back[2 * rows : 3 * rows]
-            return inner
-
-        lax.fori_loop(0, pairs, body, 0)
-        return carry
-
-    lax.fori_loop(0, chunks - 1, finish, 0)
 
     if groups > 1:
         drain(lch_r.at[0 : groups - 1], sem_x.at[2])
@@ -635,49 +663,29 @@
 
     lax.fori_loop(1, peers, share_loss, 0)
 
-    drain(rs_r, sem_x.at[4])
-
-    def add(j, summed):
-        return summed + rs_r[j].astype(F32)
-
-    ag_s[...] = lax.fori_loop(1, peers, add, rs_r[0].astype(F32)).astype(BF16)
-
-    def gather(step, carry):
-        to = lax.rem(me + step, peers)
-        push(ag_s, ag_r.at[me], sem_x.at[7], sem_x.at[8], to, ch).start()
-        return carry
-
-    pltpu.make_async_copy(ag_s, ag_r.at[me], sem_x.at[8]).start()
-    lax.fori_loop(1, peers, gather, 0)
-
-    finish(chunks - 1, 0)
+    reduce(chunks - 1)
     drain(lct_r.at[0 : peers - 1], sem_x.at[6])
 
     def add_loss(j, summed):
         return summed + lct_r[j]
 
     loss_ref[...] = lax.fori_loop(1, peers, add_loss, lct_r[0])
-    drain(ag_r, sem_x.at[8])
-
-    def emit(j, carry):
-        cols = pl.ds(pl.multiple_of(j * lanes, lanes), lanes)
-        par_b[j, 0:half_rows, :] = ag_r[2 * j].astype(F32)
-        par_b[j, half_rows:payload, :] = ag_r[2 * j + 1].astype(F32)
-        fg_ref[:, cols] = par_b[j, 0:taps, :]
-        for s in range(3):
-            sg_ref[s, :, cols] = par_b[
-                j, taps + s * short_taps : taps + (s + 1) * short_taps, :
-            ]
+
+    def arrived(c, carry):
+        drain(brecv_b.at[c], sem_br.at[c])
+        out_copy(c).wait()
         return carry
 
-    lax.fori_loop(0, col_tiles, emit, 0)
+    lax.fori_loop(0, chunks, arrived, 0)
+    drain(ag_r, sem_rr.at[1])
+    return_copy.wait()
 
     drain(meta_s.at[0:peers], sem_ms.at[0])
     for step in range(1, groups):
         loss_push(step).wait_send()
-    drain(rs_s.at[0 : peers - 1], sem_x.at[3])
+    drain(rs_s.at[0 : peers - 1], sem_rs.at[0])
     drain(lct_r.at[0 : peers - 1], sem_x.at[5])
-    drain(ag_r.at[0 : peers - 1], sem_x.at[7])
+    drain(rs_s.at[0 : peers - 1], sem_rs.at[1])
 
     def sent(c, carry):
         drain(send_b.at[c, 0:peers], sem_as.at[c])
@@ -685,6 +693,28 @@
         return carry
 
     lax.fori_loop(0, chunks, sent, 0)
+
+
+def finish_kernel(return_ref, back_ref, out_in, ag_ref, loss_in, out_ref, qg_ref, kg_ref, vg_ref, fg_ref, sg_ref, loss_ref, par_b):
+    rows = out_in.shape[0]
+    blocks, cols = back_ref.shape[1], back_ref.shape[3]
+    taps, short_taps = fg_ref.shape[0], sg_ref.shape[1]
+    half_rows = ag_ref.shape[1]
+    got = back_ref[0].reshape(blocks * block_rows, cols)
+    back = jnp.dot(return_ref[...], got, preferred_element_type=F32).astype(BF16)
+    qg_ref[...] = back[0:rows]
+    kg_ref[...] = back[rows : 2 * rows]
+    vg_ref[...] = back[2 * rows : 3 * rows]
+    out_ref[...] = out_in[...]
+    loss_ref[...] = loss_in[0:1, 0 : loss_ref.shape[1]]
+    for t in range(cols // lanes):
+        cut = slice(t * lanes, (t + 1) * lanes)
+        low = ag_ref[2 * t + 1].astype(F32)
+        fg_ref[0:half_rows, cut] = ag_ref[2 * t].astype(F32)
+        fg_ref[half_rows:taps, cut] = low[0 : taps - half_rows]
+        par_b[...] = low[taps - half_rows :]
+        for s in range(3):
+            sg_ref[s, :, cut] = par_b[s * short_taps : (s + 1) * short_taps, :]
 
 
 def shards(
@@ -711,6 +741,7 @@
     ext = rows + edge
     span = taps + ext
     payload = payload_rows(taps, short_taps)
+    share = peers // chunks
     half_rows = payload // 2
     tables = []
     made = dft_tables(rows, taps)
@@ -721,7 +752,11 @@
     vm = pltpu.VMEM
     dma = pltpu.SemaphoreType.DMA
     shape = jax.ShapeDtypeStruct
+    loaded = (query_in, key_in, value_in, target, long_filter, *tables)
     scratch = [
+        *(vm(x.shape, x.dtype) for x in loaded),
+        dma((len(loaded),)),
+        vm((rows, channels), BF16),
         vm((slots, 3 * rows), BF16),
         vm((3 * rows, slots), BF16),
         vm((slots, 3 * rows), BF16),
@@ -730,7 +765,6 @@
         vm((chunks, blocks, block_rows, width), BF16),
         vm((blocks, block_rows, lanes), BF16),
         vm((blocks, block_rows, lanes), BF16),
-        vm((chunks, blocks, block_rows, width), BF16),
         vm((chunks, blocks, block_rows, width), BF16),
         vm((3, col_tiles, rows + 2 * edge, lanes), F32),
         vm((chunks, 3, tiles, edge, lanes), BF16),
@@ -752,11 +786,10 @@
         vm((3, ext, lanes), F32),
         vm((3 * rows, 2 * lanes), BF16),
         vm((rows, lanes), F32),
-        vm((col_tiles, payload, lanes), F32),
-        vm((2 * col_tiles, half_rows, lanes), BF16),
+        vm((payload - taps, lanes), F32),
+        vm((peers, half_rows, lanes), BF16),
         vm((peers, half_rows, lanes), BF16),
         vm((half_rows, lanes), BF16),
-        vm((peers, half_rows, lanes), BF16),
         vm((8, lanes), F32),
         vm((groups, 8, lanes), F32),
         vm((8, lanes), F32),
@@ -773,23 +806,43 @@
         dma((2 * chunks,)),
         dma((1,)),
         dma((1,)),
+        dma((2,)),
+        dma((2,)),
+        dma((chunks,)),
         dma((16,)),
     ]
-    inputs = (
-        query_in,
-        key_in,
-        value_in,
+    here = pl.BlockSpec(memory_space=pltpu.VMEM)
+    away = pl.BlockSpec(memory_space=pl.ANY)
+    gated_out, brought, returning, gathered, losses = pl.pallas_call(
+        lambda *refs: whole_kernel(peers, groups, *refs),
+        out_shape=(
+            shape((rows, channels), BF16),
+            shape((chunks, blocks, block_rows, width), BF16),
+            shape((3 * rows, slots), BF16),
+            shape((peers, half_rows, lanes), BF16),
+            shape((8, lanes), F32),
+        ),
+        in_specs=[here] * 4 + [away] * len(loaded),
+        out_specs=[away] * 4 + [here],
+        scratch_shapes=scratch,
+        compiler_params=pltpu.CompilerParams(
+            collective_id=0, has_side_effects=True, vmem_limit_bytes=63_000_000
+        ),
+        name="hyena",
+    )(
         row_place.reshape(1, rows),
-        jnp.tile(row_place, 3).reshape(1, 3 * rows),
-        short_weight,
-        long_filter,
-        target,
         taxon_ids.reshape(1, rows),
         taxon_weight.reshape(1, -1),
-        *tables,
+        short_weight,
+        *loaded,
     )
+    cols = 2 * lanes
+    steps = width // cols
+    by_cols = lambda i: (0, i)
+    count = taxon_weight.shape[0]
     gated_out, query_grad, key_grad, value_grad, filter_grad, short_grad, losses = pl.pallas_call(
-        lambda *refs: whole_kernel(peers, groups, *refs),
+        finish_kernel,
+        grid=(channels // cols,),
         out_shape=(
             shape((rows, channels), BF16),
             shape((rows, channels), BF16),
@@ -797,16 +850,26 @@
             shape((rows, channels), BF16),
             shape((taps, channels), F32),
             shape((3, short_taps, channels), F32),
-            shape((8, lanes), F32),
+            shape((1, count), F32),
         ),
-        in_specs=[pl.BlockSpec(memory_space=pltpu.VMEM)] * len(inputs),
-        out_specs=[pl.BlockSpec(memory_space=pltpu.VMEM)] * 7,
-        scratch_shapes=scratch,
-        compiler_params=pltpu.CompilerParams(
-            collective_id=0, has_side_effects=True, vmem_limit_bytes=63_000_000
-        ),
-        name="hyena",
-    )(*inputs)
+        in_specs=[
+            pl.BlockSpec((3 * rows, slots), lambda i: (0, 0)),
+            pl.BlockSpec(
+                (1, blocks, block_rows, cols), lambda i: (i // steps, 0, 0, i % steps)
+            ),
+            pl.BlockSpec((rows, cols), by_cols),
+            pl.BlockSpec((2 * cols // lanes, half_rows, lanes), lambda i: (i, 0, 0)),
+            pl.BlockSpec((8, lanes), lambda i: (0, 0)),
+        ],
+        out_specs=[pl.BlockSpec((rows, cols), by_cols)] * 4
+        + [
+            pl.BlockSpec((taps, cols), by_cols),
+            pl.BlockSpec((3, short_taps, cols), lambda i: (0, 0, i)),
+            pl.BlockSpec((1, count), lambda i: (0, 0)),
+        ],
+        scratch_shapes=[vm((payload - taps, lanes), F32)],
+        name="finish",
+    )(returning, brought, gated_out, gathered, losses)
     return (
         gated_out,
         query_grad,
@@ -814,7 +877,7 @@
         value_grad,
         filter_grad,
         short_grad,
-        losses[0, : taxon_weight.shape[0]],
+        losses.reshape(count),
     )
 
 

time: 130 us -> 115 us (0.88)
  local copies, waits for them, and re-layouts: 9.37 us -> 0 us
  Pallas kernels: 120 us -> 114 us
    pallas_call x1, Pallas kernels: 120 us -> 106 us  [shards(): pl.pallas_call(lambda *refs: whole_kernel(peers, groups, *refs), out_shap...]
    unnamed x18 -> x0, local copies, waits for them, and re-layouts: 7.52 us -> none
    pallas_call x0 -> x1, Pallas kernels: none -> 7.48 us  [shards(): pl.pallas_call(finish_kernel, grid=(channels // cols,), out_shape=(shape(...]
where the time goes in v2:
time: 115 us; the launch traced here: 114 us
  Pallas kernels  114 us (99%)
    pallas_call x1, Pallas kernels, shards(): pl.pallas_call(lambda *refs: whole_kernel(peers, groups, *refs), out_shap...  106 us
    pallas_call x1, Pallas kernels, shards(): pl.pallas_call(finish_kernel, grid=(channels // cols,), out_shape=(shape(...  7.48 us

profile of v2, /device:TPU:1, one launch (start us, length us, event | category | flops | bytes accessed | tf_op | source)
XLA Modules:
  0.0 114.4 jit_solution(3063405064636952781)
XLA Ops:
  0.6 106.3 %hyena.1 = (bf16[160,2048]{1,0:T(8,128)(2,1)}, bf16[4,33,16,512]{3,2,1,0:T(8,128)(2,1)}, bf16[480,528]{1,0:T(8,128)(2,1)}, bf16[32,80,128]{2,1,0:T(8,128)(2,1)}, f32[8,128]{1,0:T(8,128)}) custom-call(s32[1,160]{1,0:T(1,128)} %bitcast.4, s32[1,160]{1,0:T(1,128)} %bitcast.5, f32[1,16]{1,0:T(1,128)} %bitcast.6, bf16[3,7,2048]{2,1,0:T(8,128)(2,1)} %refs_3_.1, ...), custom_call_target="tpu_custom_call" | custom-call | tf_op jit(solution)/shard_map/hyena/pallas_call | solution.py:816
  106.9 7.5 %finish.1 = (bf16[160,2048]{1,0:T(8,128)(2,1)}, bf16[160,2048]{1,0:T(8,128)(2,1)}, bf16[160,2048]{1,0:T(8,128)(2,1)}, bf16[160,2048]{1,0:T(8,128)(2,1)}, f32[128...) custom-call(bf16[480,528]{1,0:T(8,128)(2,1)} %get-tuple-element.19.return_ref, ...), custom_call_target="tpu_custom_call" | custom-call | tf_op jit(solution)/shard_map/finish/pallas_call | solution.py:843

commit v3 on v2

--- a/solution.py
+++ b/solution.py
@@ -81,8 +81,8 @@
     *refs,
 ):
     far = refs[:19]
-    out_hbm, brecv_b, return_hbm, ag_r, loss_ref = refs[19:24]
-    near = refs[24:43]
+    out_hbm, qg_hbm, kg_hbm, vg_hbm, ag_r, loss_ref = refs[19:25]
+    near = refs[25:44]
     (
         q_ref,
         k_ref,
@@ -104,7 +104,7 @@
         filter_hi,
         filter_lo,
     ) = near
-    sem_in = refs[43]
+    sem_in = refs[44]
     (
         out_ref,
         pack_m,
@@ -116,6 +116,8 @@
         meta_s,
         meta_r,
         bsend_b,
+        brecv_b,
+        grads_b,
         rows_b,
         prev_s,
         prev_r,
@@ -136,10 +138,15 @@
         gbuf,
         gr_b,
         lacc,
+        ids_b,
         par_b,
-        rs_s,
-        rs_r,
-        ag_s,
+        half_b,
+        half_r,
+        z_s,
+        z_r,
+        y_s,
+        y_r,
+        f_s,
         lch_s,
         lch_r,
         lct_s,
@@ -156,11 +163,17 @@
         sem_gr,
         sem_ms,
         sem_mr,
-        sem_rs,
-        sem_rr,
+        sem_hs,
+        sem_hr,
+        sem_zs,
+        sem_zr,
+        sem_ys,
+        sem_yr,
+        sem_fs,
+        sem_fr,
         sem_out,
         sem_x,
-    ) = refs[44:]
+    ) = refs[45:]
     rows, channels = q_ref.shape
     taps = filter_ref.shape[0]
     short_taps = short_ref.shape[1]
@@ -172,9 +185,14 @@
     slots = blocks * block_rows
     ext = rows + edge
     payload = payload_rows(taps, short_taps)
-    share = peers // chunks
     half_rows = payload // 2
     me = lax.axis_index("ctx")
+    depth = tiles
+    breadth = peers // (2 * depth)
+    core = lax.rem(me, 2)
+    my_y = lax.rem(me // 2, breadth)
+    my_z = me // (2 * breadth)
+    partner = me + 1 - 2 * core
     ch = lax.axis_index("ch")
     right = lax.rem(me + 1, peers)
     left = lax.rem(me + peers - 1, peers)
@@ -330,6 +348,7 @@
     taxon_hot = iota((rows, lanes), 1).astype(F32) == ids_col
     weights = jnp.concatenate([weight_ref[...], jnp.zeros((1, lanes - count), F32)], axis=1)
     weight_col = jnp.sum(jnp.where(taxon_hot, weights, 0.0), axis=1, keepdims=True)
+    ids_b[...] = jnp.broadcast_to(ids_col, (rows, lanes))
     tnext_s[...] = target_ref[0:edge, :]
     wnext_s[...] = jnp.broadcast_to(weight_col[0:edge], (edge, lanes))
     target_push.start()
@@ -339,8 +358,6 @@
             key_col + s * stream_step == slot_key_row, 1.0, 0.0
         ).astype(BF16)
 
-    return_copy = pltpu.make_async_copy(return_m, return_hbm, sem_x.at[14])
-    return_copy.start()
     for index in range(4, len(far)):
         fetch(index).wait()
 
@@ -542,9 +559,10 @@
                 lane_cut = slice(part * lanes, (part + 1) * lanes)
                 mix = mixed[:, lane_cut]
                 gg = gated_grad[:, lane_cut]
-                found_taps = taps_grad[:, lane_cut].astype(BF16)
-                rs_s[2 * at] = found_taps[0:half_rows]
-                rs_s[2 * at + 1, 0 : taps - half_rows, :] = found_taps[half_rows:]
+                tile = 2 * u + part
+                found_taps = taps_grad[:, lane_cut]
+                half_b[c, 0, tile] = found_taps[0:half_rows]
+                half_b[c, 1, tile, 0 : taps - half_rows, :] = found_taps[half_rows:]
                 out = (qc_b[at] * mix[:rows]).astype(BF16)
                 out_ref[:, cols] = out
                 lacc[...] += out.astype(F32) * target_ref[:, cols].astype(F32)
@@ -564,7 +582,7 @@
                         term = short_b[s, j : j + 1, cols] * gbuf[s, j : j + rows, :]
                         back = term if back is None else back + term
                     gr_b[s * rows : (s + 1) * rows, lane_cut] = back.astype(BF16)
-                rs_s[2 * at + 1, taps - half_rows : half_rows, :] = par_b[...].astype(BF16)
+                half_b[c, 1, tile, taps - half_rows : half_rows, :] = par_b[...]
             local = pl.ds(pl.multiple_of(u * pair_lanes, pair_lanes), pair_lanes)
             packed = jnp.dot(place_m[...], gr_b[...], preferred_element_type=F32).astype(BF16)
             bsend_b[c, :, :, local] = packed.reshape(blocks, block_rows, pair_lanes)
@@ -573,44 +591,123 @@
         lax.fori_loop(0, pairs, body, 0)
         out_copy(c).start()
 
-        def scatter(i, carry):
-            piece = c * share + i
-
-            @pl.when(piece == me)
-            def _():
-                pltpu.make_async_copy(rs_s.at[piece], rs_r.at[me], sem_rr.at[0]).start()
-
-            @pl.when(piece != me)
-            def _():
-                push(rs_s.at[piece], rs_r.at[me], sem_rs.at[0], sem_rr.at[0], piece, ch).start()
-
+        half_push(c).start()
+        exchange_back(bsend_b.at[c], brecv_b.at[c], sem_bs.at[c], sem_br.at[c])
+
+    def half_push(c):
+        return push(
+            half_b.at[c, 1 - core], half_r.at[c], sem_hs.at[c], sem_hr.at[c], partner, ch
+        )
+
+    def chip_sum(c):
+        half_push(c).wait()
+
+        def body(t, carry):
+            z_s[c, t] = (half_b[c, core, t] + half_r[c, t]).astype(BF16)
             return carry
 
-        lax.fori_loop(0, share, scatter, 0)
-        exchange_back(bsend_b.at[c], brecv_b.at[c], sem_bs.at[c], sem_br.at[c])
-
-    def reduce(c):
-        @pl.when(me // share == c)
-        def _():
-            drain(rs_r, sem_rr.at[0])
-
-            def add(j, summed):
-                return summed + rs_r[j].astype(F32)
-
-            summed = lax.fori_loop(1, peers, add, rs_r[0].astype(F32))
-            ag_s[...] = (summed * grad_scale).astype(BF16)
-
-            def gather(step, carry):
-                to = lax.rem(me + step, peers)
-                push(ag_s, ag_r.at[me], sem_rs.at[1], sem_rr.at[1], to, ch).start()
-                return carry
-
-            pltpu.make_async_copy(ag_s, ag_r.at[me], sem_rr.at[1]).start()
-            lax.fori_loop(1, peers, gather, 0)
+        lax.fori_loop(0, depth, body, 0)
+        pltpu.make_async_copy(z_s.at[c, my_z], z_r.at[c, my_z], sem_zr.at[c]).start()
+
+        def send(step, carry):
+            z_to = lax.rem(my_z + step, depth)
+            to = (z_to * breadth + my_y) * 2 + core
+            push(z_s.at[c, z_to], z_r.at[c, my_z], sem_zs.at[c], sem_zr.at[c], to, ch).start()
+            return carry
+
+        lax.fori_loop(1, depth, send, 0)
+
+    def line_sum(c):
+        drain(z_r.at[c], sem_zr.at[c])
+        summed = z_r[c, 0].astype(F32)
+        for z in range(1, depth):
+            summed = summed + z_r[c, z].astype(F32)
+        y_s[c] = summed.astype(BF16)
+        pltpu.make_async_copy(y_s.at[c], y_r.at[c, my_y], sem_yr.at[c]).start()
+
+        def send(step, carry):
+            y_to = lax.rem(my_y + step, breadth)
+            to = (my_z * breadth + y_to) * 2 + core
+            push(y_s.at[c], y_r.at[c, my_y], sem_ys.at[c], sem_yr.at[c], to, ch).start()
+            return carry
+
+        lax.fori_loop(1, breadth, send, 0)
+
+    def plane_sum(c):
+        drain(y_r.at[c], sem_yr.at[c])
+        summed = y_r[c, 0].astype(F32)
+        for y in range(1, breadth):
+            summed = summed + y_r[c, y].astype(F32)
+        f_s[c] = (summed * grad_scale).astype(BF16)
+        piece = (c * depth + my_z) * 2 + core
+        pltpu.make_async_copy(f_s.at[c], ag_r.at[piece], sem_fr.at[0]).start()
+        push(f_s.at[c], ag_r.at[piece], sem_fs.at[c], sem_fr.at[0], partner, ch).start()
+
+        def send(step, carry):
+            z_to = lax.rem(my_z + step, depth)
+            to = (z_to * breadth + my_y) * 2
+            push(f_s.at[c], ag_r.at[piece], sem_fs.at[c], sem_fr.at[0], to, ch).start()
+            push(f_s.at[c], ag_r.at[piece], sem_fs.at[c], sem_fr.at[0], to + 1, ch).start()
+            return carry
+
+        lax.fori_loop(1, depth, send, 0)
+
+    def grad_copies(c):
+        cols = pl.ds(pl.multiple_of(c * width, width), width)
+        return [
+            pltpu.make_async_copy(grads_b.at[s, :, cols], to.at[:, cols], sem_out.at[chunks + c])
+            for s, to in enumerate((qg_hbm, kg_hbm, vg_hbm))
+        ]
+
+    def finish(c):
+        drain(brecv_b.at[c], sem_br.at[c])
+
+        def body(u, inner):
+            local = pl.ds(pl.multiple_of(u * pair_lanes, pair_lanes), pair_lanes)
+            cols = pl.ds(pl.multiple_of(c * width + u * pair_lanes, pair_lanes), pair_lanes)
+            got = brecv_b[c, :, :, local].reshape(slots, pair_lanes)
+            back = jnp.dot(return_m[...], got, preferred_element_type=F32).astype(BF16)
+            for s in range(3):
+                grads_b[s, :, cols] = back[s * rows : (s + 1) * rows]
+            return inner
+
+        lax.fori_loop(0, pairs, body, 0)
+        for copy in grad_copies(c):
+            copy.start()
 
     def out_copy(c):
         cols = pl.ds(pl.multiple_of(c * width, width), width)
         return pltpu.make_async_copy(out_ref.at[:, cols], out_hbm.at[:, cols], sem_out.at[c])
+
+    def loss_push(step):
+        return push(
+            lch_s, lch_r.at[ch], sem_x.at[8 + step], sem_x.at[2], me, lax.rem(ch + step, groups)
+        )
+
+    def start_loss():
+        row_loss = jnp.sum(lacc[...], axis=1, keepdims=True)
+        hot = iota((rows, lanes), 1).astype(F32) == ids_b[...]
+        taxon_part = jnp.sum(jnp.where(hot, row_loss, 0.0), axis=0, keepdims=True) * loss_scale
+        lch_s[...] = jnp.broadcast_to(taxon_part, (8, lanes))
+        lch_r[ch] = jnp.broadcast_to(taxon_part, (8, lanes))
+        for step in range(1, groups):
+            loss_push(step).start()
+
+    def share_loss():
+        if groups > 1:
+            drain(lch_r.at[0 : groups - 1], sem_x.at[2])
+        total = lch_r[0]
+        for g in range(1, groups):
+            total = total + lch_r[g]
+        lct_s[...] = total
+        lct_r[me] = total
+
+        def send(step, carry):
+            to = lax.rem(me + step, peers)
+            push(lct_s, lct_r.at[me], sem_x.at[5], sem_x.at[6], to, ch).start()
+            return carry
+
+        lax.fori_loop(1, peers, send, 0)
 
     def steps(t, carry):
         @pl.when(t < chunks)
@@ -621,93 +718,83 @@
         def _():
             convolve(t - 1)
 
-        @pl.when(t >= 2)
+        @pl.when(jnp.logical_and(t >= 3, t < chunks + 3))
+        def _():
+            chip_sum(t - 3)
+
+        @pl.when(jnp.logical_and(t >= 4, t < chunks + 4))
+        def _():
+            line_sum(t - 4)
+
+        @pl.when(t >= 5)
+        def _():
+            plane_sum(t - 5)
+
+        @pl.when(jnp.logical_and(t >= 2, t < chunks + 2))
         def _():
             backward(t - 2)
 
-        @pl.when(t >= 3)
+        @pl.when(t == chunks + 1)
         def _():
-            reduce(t - 3)
+            start_loss()
+
+        @pl.when(t == chunks + 2)
+        def _():
+            share_loss()
+
+        @pl.when(t >= 5)
+        def _():
+            finish(t - 5)
 
         return carry
 
-    lax.fori_loop(0, chunks + 2, steps, 0)
-
-    row_loss = jnp.sum(lacc[...], axis=1, keepdims=True)
-    taxon_part = (
-        jnp.sum(jnp.where(taxon_hot[0:rows], row_loss, 0.0), axis=0, keepdims=True) * loss_scale
-    )
-    lch_s[...] = jnp.broadcast_to(taxon_part, (8, lanes))
-    lch_r[ch] = jnp.broadcast_to(taxon_part, (8, lanes))
-
-    def loss_push(step):
-        return push(
-            lch_s, lch_r.at[ch], sem_x.at[8 + step], sem_x.at[2], me, lax.rem(ch + step, groups)
-        )
-
-    for step in range(1, groups):
-        loss_push(step).start()
-
-    if groups > 1:
-        drain(lch_r.at[0 : groups - 1], sem_x.at[2])
-    total = lch_r[0]
-    for g in range(1, groups):
-        total = total + lch_r[g]
-    lct_s[...] = total
-    lct_r[me] = total
-
-    def share_loss(step, carry):
-        to = lax.rem(me + step, peers)
-        push(lct_s, lct_r.at[me], sem_x.at[5], sem_x.at[6], to, ch).start()
-        return carry
-
-    lax.fori_loop(1, peers, share_loss, 0)
-
-    reduce(chunks - 1)
+    lax.fori_loop(0, chunks + 5, steps, 0)
+
     drain(lct_r.at[0 : peers - 1], sem_x.at[6])
 
     def add_loss(j, summed):
         return summed + lct_r[j]
 
     loss_ref[...] = lax.fori_loop(1, peers, add_loss, lct_r[0])
-
-    def arrived(c, carry):
-        drain(brecv_b.at[c], sem_br.at[c])
+    for c in range(chunks):
         out_copy(c).wait()
-        return carry
-
-    lax.fori_loop(0, chunks, arrived, 0)
-    drain(ag_r, sem_rr.at[1])
-    return_copy.wait()
+        for copy in grad_copies(c):
+            copy.wait()
+    drain(ag_r, sem_fr.at[0])
 
     drain(meta_s.at[0:peers], sem_ms.at[0])
     for step in range(1, groups):
         loss_push(step).wait_send()
-    drain(rs_s.at[0 : peers - 1], sem_rs.at[0])
     drain(lct_r.at[0 : peers - 1], sem_x.at[5])
-    drain(rs_s.at[0 : peers - 1], sem_rs.at[1])
 
     def sent(c, carry):
         drain(send_b.at[c, 0:peers], sem_as.at[c])
         drain(bsend_b.at[c, 0:peers], sem_bs.at[c])
+        drain(z_r.at[c, 0 : depth - 1], sem_zs.at[c])
+        drain(y_r.at[c, 0 : breadth - 1], sem_ys.at[c])
+        drain(ag_r.at[0 : 2 * depth - 1], sem_fs.at[c])
         return carry
 
     lax.fori_loop(0, chunks, sent, 0)
 
 
-def finish_kernel(return_ref, back_ref, out_in, ag_ref, loss_in, out_ref, qg_ref, kg_ref, vg_ref, fg_ref, sg_ref, loss_ref, par_b):
-    rows = out_in.shape[0]
-    blocks, cols = back_ref.shape[1], back_ref.shape[3]
+def finish_kernel(*refs):
+    sources, loss_in = refs[0:5], refs[5]
+    targets, loss_ref = refs[6:12], refs[12]
+    held, par_b, sem_in, sem_out = refs[13:20], refs[20], refs[21], refs[22]
+    ag_ref, fg_ref, sg_ref = held[4:7]
     taps, short_taps = fg_ref.shape[0], sg_ref.shape[1]
     half_rows = ag_ref.shape[1]
-    got = back_ref[0].reshape(blocks * block_rows, cols)
-    back = jnp.dot(return_ref[...], got, preferred_element_type=F32).astype(BF16)
-    qg_ref[...] = back[0:rows]
-    kg_ref[...] = back[rows : 2 * rows]
-    vg_ref[...] = back[2 * rows : 3 * rows]
-    out_ref[...] = out_in[...]
+    ins = [pltpu.make_async_copy(sources[i], held[i], sem_in.at[i]) for i in range(5)]
+    leaving = (0, 1, 2, 3, 5, 6)
+    outs = [
+        pltpu.make_async_copy(held[i], targets[n], sem_out.at[n]) for n, i in enumerate(leaving)
+    ]
+    for i in (4, 0, 1, 2, 3):
+        ins[i].start()
     loss_ref[...] = loss_in[0:1, 0 : loss_ref.shape[1]]
-    for t in range(cols // lanes):
+    ins[4].wait()
+    for t in range(fg_ref.shape[1] // lanes):
         cut = slice(t * lanes, (t + 1) * lanes)
         low = ag_ref[2 * t + 1].astype(F32)
         fg_ref[0:half_rows, cut] = ag_ref[2 * t].astype(F32)
@@ -715,6 +802,13 @@
         par_b[...] = low[taps - half_rows :]
         for s in range(3):
             sg_ref[s, :, cut] = par_b[s * short_taps : (s + 1) * short_taps, :]
+    outs[4].start()
+    outs[5].start()
+    for i in range(4):
+        ins[i].wait()
+        outs[i].start()
+    for copy in outs:
+        copy.wait()
 
 
 def shards(
@@ -741,7 +835,6 @@
     ext = rows + edge
     span = taps + ext
     payload = payload_rows(taps, short_taps)
-    share = peers // chunks
     half_rows = payload // 2
     tables = []
     made = dft_tables(rows, taps)
@@ -766,6 +859,8 @@
         vm((blocks, block_rows, lanes), BF16),
         vm((blocks, block_rows, lanes), BF16),
         vm((chunks, blocks, block_rows, width), BF16),
+        vm((chunks, blocks, block_rows, width), BF16),
+        vm((3, rows, channels), BF16),
         vm((3, col_tiles, rows + 2 * edge, lanes), F32),
         vm((chunks, 3, tiles, edge, lanes), BF16),
         vm((chunks, 3, tiles, edge, lanes), BF16),
@@ -786,10 +881,15 @@
         vm((3, ext, lanes), F32),
         vm((3 * rows, 2 * lanes), BF16),
         vm((rows, lanes), F32),
+        vm((rows, lanes), F32),
         vm((payload - taps, lanes), F32),
-        vm((peers, half_rows, lanes), BF16),
-        vm((peers, half_rows, lanes), BF16),
-        vm((half_rows, lanes), BF16),
+        vm((chunks, 2, tiles, half_rows, lanes), F32),
+        vm((chunks, tiles, half_rows, lanes), F32),
+        vm((chunks, tiles, half_rows, lanes), BF16),
+        vm((chunks, tiles, half_rows, lanes), BF16),
+        vm((chunks, half_rows, lanes), BF16),
+        vm((chunks, peers // (2 * tiles), half_rows, lanes), BF16),
+        vm((chunks, half_rows, lanes), BF16),
         vm((8, lanes), F32),
         vm((groups, 8, lanes), F32),
         vm((8, lanes), F32),
@@ -806,24 +906,28 @@
         dma((2 * chunks,)),
         dma((1,)),
         dma((1,)),
-        dma((2,)),
-        dma((2,)),
-        dma((chunks,)),
+        dma((chunks,)),
+        dma((chunks,)),
+        dma((chunks,)),
+        dma((chunks,)),
+        dma((chunks,)),
+        dma((chunks,)),
+        dma((chunks,)),
+        dma((1,)),
+        dma((2 * chunks,)),
         dma((16,)),
     ]
     here = pl.BlockSpec(memory_space=pltpu.VMEM)
     away = pl.BlockSpec(memory_space=pl.ANY)
-    gated_out, brought, returning, gathered, losses = pl.pallas_call(
+    *moved, gathered, losses = pl.pallas_call(
         lambda *refs: whole_kernel(peers, groups, *refs),
         out_shape=(
-            shape((rows, channels), BF16),
-            shape((chunks, blocks, block_rows, width), BF16),
-            shape((3 * rows, slots), BF16),
+            *(shape((rows, channels), BF16) for _ in range(4)),
             shape((peers, half_rows, lanes), BF16),
             shape((8, lanes), F32),
         ),
         in_specs=[here] * 4 + [away] * len(loaded),
-        out_specs=[away] * 4 + [here],
+        out_specs=[away] * 5 + [here],
         scratch_shapes=scratch,
         compiler_params=pltpu.CompilerParams(
             collective_id=0, has_side_effects=True, vmem_limit_bytes=63_000_000
@@ -836,40 +940,28 @@
         short_weight,
         *loaded,
     )
-    cols = 2 * lanes
-    steps = width // cols
-    by_cols = lambda i: (0, i)
     count = taxon_weight.shape[0]
     gated_out, query_grad, key_grad, value_grad, filter_grad, short_grad, losses = pl.pallas_call(
         finish_kernel,
-        grid=(channels // cols,),
         out_shape=(
-            shape((rows, channels), BF16),
-            shape((rows, channels), BF16),
-            shape((rows, channels), BF16),
-            shape((rows, channels), BF16),
+            *(shape((rows, channels), BF16) for _ in range(4)),
             shape((taps, channels), F32),
             shape((3, short_taps, channels), F32),
             shape((1, count), F32),
         ),
-        in_specs=[
-            pl.BlockSpec((3 * rows, slots), lambda i: (0, 0)),
-            pl.BlockSpec(
-                (1, blocks, block_rows, cols), lambda i: (i // steps, 0, 0, i % steps)
-            ),
-            pl.BlockSpec((rows, cols), by_cols),
-            pl.BlockSpec((2 * cols // lanes, half_rows, lanes), lambda i: (i, 0, 0)),
-            pl.BlockSpec((8, lanes), lambda i: (0, 0)),
+        in_specs=[away] * 5 + [here],
+        out_specs=[away] * 6 + [here],
+        scratch_shapes=[
+            *(vm((rows, channels), BF16) for _ in range(4)),
+            vm((peers, half_rows, lanes), BF16),
+            vm((taps, channels), F32),
+            vm((3, short_taps, channels), F32),
+            vm((payload - taps, lanes), F32),
+            dma((5,)),
+            dma((6,)),
         ],
-        out_specs=[pl.BlockSpec((rows, cols), by_cols)] * 4
-        + [
-            pl.BlockSpec((taps, cols), by_cols),
-            pl.BlockSpec((3, short_taps, cols), lambda i: (0, 0, i)),
-            pl.BlockSpec((1, count), lambda i: (0, 0)),
-        ],
-        scratch_shapes=[vm((payload - taps, lanes), F32)],
         name="finish",
-    )(returning, brought, gated_out, gathered, losses)
+    )(*moved, gathered, losses)
     return (
         gated_out,
         query_grad,

time: 115 us -> 103 us (0.90)
  Pallas kernels: 114 us -> 102 us
    pallas_call x1, Pallas kernels: 106 us -> 97.3 us  [shards(): pl.pallas_call(lambda *refs: whole_kernel(peers, groups, *refs), out_shap...]
    pallas_call x1, Pallas kernels: 7.48 us -> 4.4 us  [shards(): pl.pallas_call(finish_kernel, out_shape=(*(shape((rows, channels), BF16)...]
where the time goes in v3:
time: 103 us; the launch traced here: 102 us
  Pallas kernels  102 us (99%)
    pallas_call x1, Pallas kernels, shards(): pl.pallas_call(lambda *refs: whole_kernel(peers, groups, *refs), out_shap...  97.3 us
    pallas_call x1, Pallas kernels, shards(): pl.pallas_call(finish_kernel, out_shape=(*(shape((rows, channels), BF16)...  4.4 us

profile of v3, /device:TPU:1, one launch (start us, length us, event | category | flops | bytes accessed | tf_op | source)
XLA Modules:
  0.0 102.4 jit_solution(12007721743920358464)
XLA Ops:
  0.6 97.3 %hyena.1 = (bf16[160,2048]{1,0:T(8,128)(2,1)}, bf16[160,2048]{1,0:T(8,128)(2,1)}, bf16[160,2048]{1,0:T(8,128)(2,1)}, bf16[160,2048]{1,0:T(8,128)(2,1)}, bf16[32,80,128]{2,1,0:T(8,128)(2,1)}, /*index=5*/f32[8,128]{1,0:T(8,128)}) custom-call(s32[1,160]{1,0:T(1,128)} %bitcast.4, s32[1,160]{1,0:T(1,128)} %bitcast.5, f32[1,16]{1,0:T(1,128)} %bitcast.6, ...), custom_call_target="tpu_custom_call" | custom-call | tf_op jit(solution)/shard_map/hyena/pallas_call | solution.py:922
  98.0 4.4 %finish.1 = (bf16[160,2048]{1,0:T(8,128)(2,1)}, bf16[160,2048]{1,0:T(8,128)(2,1)}, bf16[160,2048]{1,0:T(8,128)(2,1)}, bf16[160,2048]{1,0:T(8,128)(2,1)}, f32[128...) custom-call(bf16[160,2048]{1,0:T(8,128)(2,1)} %get-tuple-element.20.refs_0_, ...), custom_call_target="tpu_custom_call" | custom-call | tf_op jit(solution)/shard_map/finish/pallas_call | solution.py:944

commit v4 on v3

--- a/solution.py
+++ b/solution.py
@@ -16,6 +16,7 @@
 lanes = 128
 edge = 16
 chunks = 4
+window = 2
 stream_step = 1024.0
 
 
@@ -315,16 +316,25 @@
 
         lax.fori_loop(1, peers, body, 0)
 
-    def exchange_back(source, landing, send_sem, recv_sem):
-        pltpu.make_async_copy(source.at[me], landing.at[me], recv_sem).start()
-        push(source.at[peers], landing.at[peers], send_sem, recv_sem, left, ch).start()
-
+    near_peers = peers // 2
+
+    def return_some(c, first, last):
         def body(step, carry):
             to = lax.rem(me + step, peers)
-            push(source.at[to], landing.at[me], send_sem, recv_sem, to, ch).start()
+            push(bsend_b.at[c, to], brecv_b.at[c, me], sem_bs.at[c], sem_br.at[c], to, ch).start()
             return carry
 
-        lax.fori_loop(1, peers, body, 0)
+        lax.fori_loop(first, last, body, 0)
+
+    def return_first(c):
+        pltpu.make_async_copy(bsend_b.at[c, me], brecv_b.at[c, me], sem_br.at[c]).start()
+        push(
+            bsend_b.at[c, peers], brecv_b.at[c, peers], sem_bs.at[c], sem_br.at[c], left, ch
+        ).start()
+        return_some(c, 1, near_peers)
+
+    def return_rest(c):
+        return_some(c, near_peers, peers)
 
     for index in range(3):
         fetch(index).wait()
@@ -340,7 +350,7 @@
         exchange(send_b.at[c], recv_b.at[c], sem_as.at[c], sem_ar.at[c])
         return carry
 
-    lax.fori_loop(1, chunks, pack_and_send, 0)
+    lax.fori_loop(1, window, pack_and_send, 0)
     fetch(3).wait()
     ids_row = taxon_ref[...].astype(F32)
     ids_col = column(ids_row, rows)
@@ -358,6 +368,7 @@
             key_col + s * stream_step == slot_key_row, 1.0, 0.0
         ).astype(BF16)
 
+    lax.fori_loop(window, chunks, pack, 0)
     for index in range(4, len(far)):
         fetch(index).wait()
 
@@ -592,7 +603,6 @@
         out_copy(c).start()
 
         half_push(c).start()
-        exchange_back(bsend_b.at[c], brecv_b.at[c], sem_bs.at[c], sem_br.at[c])
 
     def half_push(c):
         return push(
@@ -675,6 +685,10 @@
         for copy in grad_copies(c):
             copy.start()
 
+    def finish_step(c, carry):
+        finish(c)
+        return carry
+
     def out_copy(c):
         cols = pl.ds(pl.multiple_of(c * width, width), width)
         return pltpu.make_async_copy(out_ref.at[:, cols], out_hbm.at[:, cols], sem_out.at[c])
@@ -718,11 +732,11 @@
         def _():
             convolve(t - 1)
 
-        @pl.when(jnp.logical_and(t >= 3, t < chunks + 3))
+        @pl.when(t >= 3)
         def _():
             chip_sum(t - 3)
 
-        @pl.when(jnp.logical_and(t >= 4, t < chunks + 4))
+        @pl.when(t >= 4)
         def _():
             line_sum(t - 4)
 
@@ -730,25 +744,42 @@
         def _():
             plane_sum(t - 5)
 
-        @pl.when(jnp.logical_and(t >= 2, t < chunks + 2))
+        @pl.when(t + window < chunks)
+        def _():
+            later = t + window
+            exchange(send_b.at[later], recv_b.at[later], sem_as.at[later], sem_ar.at[later])
+
+        @pl.when(t >= 3)
+        def _():
+            return_rest(t - 3)
+
+        @pl.when(t >= 2)
         def _():
             backward(t - 2)
 
         @pl.when(t == chunks + 1)
         def _():
-            start_loss()
-
-        @pl.when(t == chunks + 2)
-        def _():
-            share_loss()
-
-        @pl.when(t >= 5)
-        def _():
-            finish(t - 5)
+            chip_sum(t - 2)
+
+        @pl.when(t >= 2)
+        def _():
+            return_first(t - 2)
 
         return carry
 
-    lax.fori_loop(0, chunks + 5, steps, 0)
+    lax.fori_loop(0, chunks + 2, steps, 0)
+    last = chunks - 1
+    start_loss()
+    line_sum(last - 1)
+    plane_sum(last - 2)
+    finish(0)
+    line_sum(last)
+    return_rest(last)
+    share_loss()
+    plane_sum(last - 1)
+    finish(1)
+    plane_sum(last)
+    lax.fori_loop(2, chunks, finish_step, 0)
 
     drain(lct_r.at[0 : peers - 1], sem_x.at[6])
 

time: 103 us -> 92.8 us (0.901)
  Pallas kernels: 102 us -> 92 us
    pallas_call x1, Pallas kernels: 97.3 us -> 87.6 us  [shards(): pl.pallas_call(lambda *refs: whole_kernel(peers, groups, *refs), out_shap...]
where the time goes in v4:
time: 92.8 us; the launch traced here: 92.6 us
  Pallas kernels  92 us (99%)
    pallas_call x1, Pallas kernels, shards(): pl.pallas_call(lambda *refs: whole_kernel(peers, groups, *refs), out_shap...  87.6 us
    pallas_call x1, Pallas kernels, shards(): pl.pallas_call(finish_kernel, out_shape=(*(shape((rows, channels), BF16)...  4.4 us

profile of v4, /device:TPU:1, one launch (start us, length us, event | category | flops | bytes accessed | tf_op | source)
XLA Modules:
  0.0 92.6 jit_solution(15976695609646842480)
XLA Ops:
  0.6 87.6 %hyena.1 = (bf16[160,2048]{1,0:T(8,128)(2,1)}, bf16[160,2048]{1,0:T(8,128)(2,1)}, bf16[160,2048]{1,0:T(8,128)(2,1)}, bf16[160,2048]{1,0:T(8,128)(2,1)}, bf16[32,80,128]{2,1,0:T(8,128)(2,1)}, /*index=5*/f32[8,128]{1,0:T(8,128)}) custom-call(s32[1,160]{1,0:T(1,128)} %bitcast.4, s32[1,160]{1,0:T(1,128)} %bitcast.5, f32[1,16]{1,0:T(1,128)} %bitcast.6, ...), custom_call_target="tpu_custom_call" | custom-call | tf_op jit(solution)/shard_map/hyena/pallas_call | solution.py:953
  88.2 4.4 %finish.1 = (bf16[160,2048]{1,0:T(8,128)(2,1)}, bf16[160,2048]{1,0:T(8,128)(2,1)}, bf16[160,2048]{1,0:T(8,128)(2,1)}, bf16[160,2048]{1,0:T(8,128)(2,1)}, f32[128...) custom-call(bf16[160,2048]{1,0:T(8,128)(2,1)} %get-tuple-element.20.refs_0_, ...), custom_call_target="tpu_custom_call" | custom-call | tf_op jit(solution)/shard_map/finish/pallas_call | solution.py:975

commit v5 on v4

--- a/solution.py
+++ b/solution.py
@@ -16,6 +16,7 @@
 lanes = 128
 edge = 16
 chunks = 4
+stride = 7
 window = 2
 stream_step = 1024.0
 
@@ -52,6 +53,7 @@
     return tables
 
 
+back_names = ("mixed", "gated", "filter")
 table_names = ("taps", "ahead", "own", "later", "mixed", "gated", "filter")
 
 
@@ -81,31 +83,24 @@
     short_ref,
     *refs,
 ):
-    far = refs[:19]
-    out_hbm, qg_hbm, kg_hbm, vg_hbm, ag_r, loss_ref = refs[19:25]
-    near = refs[25:44]
+    far = refs[:12]
+    out_hbm, qg_hbm, kg_hbm, vg_hbm, ag_r, loss_ref = refs[12:18]
+    near = refs[18:30]
     (
         q_ref,
         k_ref,
         v_ref,
         target_ref,
         filter_ref,
-        taps_hi,
-        taps_lo,
-        ahead_hi,
-        ahead_lo,
-        own_hi,
-        own_lo,
-        later_hi,
-        later_lo,
-        mixed_hi,
-        mixed_lo,
-        gated_hi,
-        gated_lo,
-        filter_hi,
-        filter_lo,
+        taps_t,
+        ahead_t,
+        own_t,
+        later_t,
+        mixed_t,
+        gated_t,
+        filter_t,
     ) = near
-    sem_in = refs[44]
+    sem_in = refs[30]
     (
         out_ref,
         pack_m,
@@ -174,7 +169,7 @@
         sem_fr,
         sem_out,
         sem_x,
-    ) = refs[45:]
+    ) = refs[31:]
     rows, channels = q_ref.shape
     taps = filter_ref.shape[0]
     short_taps = short_ref.shape[1]
@@ -310,7 +305,7 @@
         push(source.at[peers], landing.at[peers], send_sem, recv_sem, right, ch).start()
 
         def body(step, carry):
-            to = lax.rem(me + step, peers)
+            to = lax.rem(me + step * stride, peers)
             push(source.at[to], landing.at[me], send_sem, recv_sem, to, ch).start()
             return carry
 
@@ -320,7 +315,7 @@
 
     def return_some(c, first, last):
         def body(step, carry):
-            to = lax.rem(me + step, peers)
+            to = lax.rem(me + step * stride, peers)
             push(bsend_b.at[c, to], brecv_b.at[c, me], sem_bs.at[c], sem_br.at[c], to, ch).start()
             return carry
 
@@ -374,12 +369,15 @@
 
     short_b[:, 0:short_taps, :] = short_ref[...].astype(F32)
 
+    def both(table, x):
+        return jnp.dot(
+            table[...], jnp.concatenate([x, x], axis=0), preferred_element_type=F32
+        )
+
     def filter_spectrum(u, carry):
         cols = pl.ds(pl.multiple_of(u * pair_lanes, pair_lanes), pair_lanes)
         x = filter_ref[:, cols]
-        found = jnp.dot(taps_hi[...], x, preferred_element_type=F32) + jnp.dot(
-            taps_lo[...], x, preferred_element_type=F32
-        )
+        found = both(taps_t, x)
         spec_b[2 * u] = found[:, :lanes]
         spec_b[2 * u + 1] = found[:, lanes:]
         return carry
@@ -505,18 +503,12 @@
         gated_push(c).start()
         mixed_push(c).start()
 
-    def both(high, low, x):
-        return jnp.dot(high, x, preferred_element_type=F32) + jnp.dot(
-            low, x, preferred_element_type=F32
-        )
-
-    def inverse(high, low, real, imag):
+    def inverse(table, real, imag):
         y = jnp.concatenate([real, imag], axis=0)
         y_hi = y.astype(BF16)
         y_lo = (y - y_hi.astype(F32)).astype(BF16)
-        return both(high[...], low[...], y_hi) + jnp.dot(
-            high[...], y_lo, preferred_element_type=F32
-        )
+        stacked = jnp.concatenate([y_hi, y_lo, y_hi], axis=0)
+        return jnp.dot(table[...], stacked, preferred_element_type=F32)
 
     def backward(c):
         gated_push(c).wait()
@@ -555,15 +547,15 @@
             )
             spec = jnp.concatenate([spec_b[first], spec_b[first + 1]], axis=1)
             fr, fi = spec[:rows], spec[rows:]
-            sg = both(ahead_hi[...], ahead_lo[...], gx)
+            sg = both(ahead_t, gx)
             gr, gi = sg[:rows], sg[rows:]
-            mixed = inverse(mixed_hi, mixed_lo, fr * gr - fi * gi, fr * gi + fi * gr)
-            so = both(own_hi[...], own_lo[...], g_own)
+            mixed = inverse(mixed_t, fr * gr - fi * gi, fr * gi + fi * gr)
+            so = both(own_t, g_own)
             mr, mi = so[:rows], so[rows:]
-            taps_grad = inverse(filter_hi, filter_lo, mr * gr + mi * gi, mr * gi - mi * gr)
-            sl = both(later_hi[...], later_lo[...], g_later)
+            taps_grad = inverse(filter_t, mr * gr + mi * gi, mr * gi - mi * gr)
+            sl = both(later_t, g_later)
             ar, ai = mr + sl[:rows], mi + sl[rows:]
-            gated_grad = inverse(gated_hi, gated_lo, fr * ar + fi * ai, fr * ai - fi * ar)
+            gated_grad = inverse(gated_t, fr * ar + fi * ai, fr * ai - fi * ar)
             for part in range(2):
                 at = first + part
                 cols = pl.ds(pl.multiple_of(at * lanes, lanes), lanes)
@@ -581,16 +573,13 @@
                 gbuf[1] = gg * vc_b[at]
                 gbuf[2] = gg * kc_b[at]
                 for s in range(3):
-                    own = gbuf[s, 0:rows, :]
+                    own = rows_b[s, at, edge : edge + rows, :]
                     back = None
                     for j in range(short_taps):
-                        found = jnp.sum(
-                            own * rows_b[s, at, edge - j : edge - j + rows, :],
-                            axis=0,
-                            keepdims=True,
-                        )
+                        ahead = gbuf[s, j : j + rows, :]
+                        found = jnp.sum(ahead * own, axis=0, keepdims=True)
                         par_b[s * short_taps + j : s * short_taps + j + 1, :] = found
-                        term = short_b[s, j : j + 1, cols] * gbuf[s, j : j + rows, :]
+                        term = short_b[s, j : j + 1, cols] * ahead
                         back = term if back is None else back + term
                     gr_b[s * rows : (s + 1) * rows, lane_cut] = back.astype(BF16)
                 half_b[c, 1, tile, taps - half_rows : half_rows, :] = par_b[...]
@@ -871,8 +860,8 @@
     made = dft_tables(rows, taps)
     for name in table_names:
         high, low = split_constant(made[name])
-        tables.append(jnp.asarray(high))
-        tables.append(jnp.asarray(low))
+        parts = (high, high, low) if name in back_names else (high, low)
+        tables.append(jnp.asarray(np.concatenate(parts, axis=1)))
     vm = pltpu.VMEM
     dma = pltpu.SemaphoreType.DMA
     shape = jax.ShapeDtypeStruct

time: 92.8 us -> 89 us (0.959)
  Pallas kernels: 92 us -> 88.1 us
    pallas_call x1, Pallas kernels: 87.6 us -> 83.7 us  [shards(): pl.pallas_call(lambda *refs: whole_kernel(peers, groups, *refs), out_shap...]
where the time goes in v5:
time: 89 us; the launch traced here: 88.8 us
  Pallas kernels  88.1 us (99%)
    pallas_call x1, Pallas kernels, shards(): pl.pallas_call(lambda *refs: whole_kernel(peers, groups, *refs), out_shap...  83.7 us
    pallas_call x1, Pallas kernels, shards(): pl.pallas_call(finish_kernel, out_shape=(*(shape((rows, channels), BF16)...  4.4 us

profile of v5, /device:TPU:1, one launch (start us, length us, event | category | flops | bytes accessed | tf_op | source)
XLA Modules:
  0.0 88.8 jit_solution(14953129646917702984)
XLA Ops:
  0.6 83.7 %hyena.1 = (bf16[160,2048]{1,0:T(8,128)(2,1)}, bf16[160,2048]{1,0:T(8,128)(2,1)}, bf16[160,2048]{1,0:T(8,128)(2,1)}, bf16[160,2048]{1,0:T(8,128)(2,1)}, bf16[32,80,128]{2,1,0:T(8,128)(2,1)}, /*index=5*/f32[8,128]{1,0:T(8,128)}) custom-call(s32[1,160]{1,0:T(1,128)} %bitcast.4, s32[1,160]{1,0:T(1,128)} %bitcast.5, f32[1,16]{1,0:T(1,128)} %bitcast.6, ...), custom_call_target="tpu_custom_call" | custom-call | tf_op jit(solution)/shard_map/hyena/pallas_call | solution.py:942
  84.4 4.4 %finish.1 = (bf16[160,2048]{1,0:T(8,128)(2,1)}, bf16[160,2048]{1,0:T(8,128)(2,1)}, bf16[160,2048]{1,0:T(8,128)(2,1)}, bf16[160,2048]{1,0:T(8,128)(2,1)}, f32[128...) custom-call(bf16[160,2048]{1,0:T(8,128)(2,1)} %get-tuple-element.20.refs_0_, ...), custom_call_target="tpu_custom_call" | custom-call | tf_op jit(solution)/shard_map/finish/pallas_call | solution.py:964

commit v6 on v5

--- a/solution.py
+++ b/solution.py
@@ -311,7 +311,7 @@
 
         lax.fori_loop(1, peers, body, 0)
 
-    near_peers = peers // 2
+    near_peers = 3 * peers // 4
 
     def return_some(c, first, last):
         def body(step, carry):
@@ -810,9 +810,11 @@
     outs = [
         pltpu.make_async_copy(held[i], targets[n], sem_out.at[n]) for n, i in enumerate(leaving)
     ]
-    for i in (4, 0, 1, 2, 3):
+    for i in (0, 4, 1, 2, 3):
         ins[i].start()
     loss_ref[...] = loss_in[0:1, 0 : loss_ref.shape[1]]
+    ins[0].wait()
+    outs[0].start()
     ins[4].wait()
     for t in range(fg_ref.shape[1] // lanes):
         cut = slice(t * lanes, (t + 1) * lanes)
@@ -824,7 +826,7 @@
             sg_ref[s, :, cut] = par_b[s * short_taps : (s + 1) * short_taps, :]
     outs[4].start()
     outs[5].start()
-    for i in range(4):
+    for i in range(1, 4):
         ins[i].wait()
         outs[i].start()
     for copy in outs:

time: 89 us -> 89.5 us (level)
  no operation moved by 1% of the time
where the time goes in v6:
time: 89.5 us; the launch traced here: 89.4 us
  Pallas kernels  88.7 us (99%)
    pallas_call x1, Pallas kernels, shards(): pl.pallas_call(lambda *refs: whole_kernel(peers, groups, *refs), out_shap...  84.3 us
    pallas_call x1, Pallas kernels, shards(): pl.pallas_call(finish_kernel, out_shape=(*(shape((rows, channels), BF16)...  4.38 us

profile of v6, /device:TPU:1, one launch (start us, length us, event | category | flops | bytes accessed | tf_op | source)
XLA Modules:
  0.0 89.4 jit_solution(17232729472391078980)
XLA Ops:
  0.6 84.3 %hyena.1 = (bf16[160,2048]{1,0:T(8,128)(2,1)}, bf16[160,2048]{1,0:T(8,128)(2,1)}, bf16[160,2048]{1,0:T(8,128)(2,1)}, bf16[160,2048]{1,0:T(8,128)(2,1)}, bf16[32,80,128]{2,1,0:T(8,128)(2,1)}, /*index=5*/f32[8,128]{1,0:T(8,128)}) custom-call(s32[1,160]{1,0:T(1,128)} %bitcast.4, s32[1,160]{1,0:T(1,128)} %bitcast.5, f32[1,16]{1,0:T(1,128)} %bitcast.6, ...), custom_call_target="tpu_custom_call" | custom-call | tf_op jit(solution)/shard_map/hyena/pallas_call | solution.py:944
  85.0 4.4 %finish.1 = (bf16[160,2048]{1,0:T(8,128)(2,1)}, bf16[160,2048]{1,0:T(8,128)(2,1)}, bf16[160,2048]{1,0:T(8,128)(2,1)}, bf16[160,2048]{1,0:T(8,128)(2,1)}, f32[128...) custom-call(bf16[160,2048]{1,0:T(8,128)(2,1)} %get-tuple-element.20.refs_0_, ...), custom_call_target="tpu_custom_call" | custom-call | tf_op jit(solution)/shard_map/finish/pallas_call | solution.py:966
